TPU v7x, 128 devices: a whole 4x4x4 slice. The times are simulated.
128 devices in a mesh: shard: 128 (over z, x, y, core).
Axes of the slice: x: 4, y: 4, z: 4, core: 2. Of those that a mesh axis runs over, the one named last changes fastest.
Arguments:
- queries: bfloat16 [2048, 8, 9600], P('shard'), may hold values from -6 to 6
- index_videos: bfloat16 [16384, 8, 9600], P('shard'), may hold values from -6 to 6
- candidates: int32 [2048, 8], P('shard'), may hold values from 0 to 16383, as said below
- conv_one: bfloat16 [32, 1, 3, 3], replicated, may hold values from -2 to 2
- conv_two: bfloat16 [64, 32, 3, 3], replicated, may hold values from -0.375 to 0.375
- conv_three: bfloat16 [1, 64, 3, 3], replicated, may hold values from -0.25 to 0.25
Outputs:
- scores: float32 [2048, 8], P('shard')
Inputs may be any that keep to these rules, and one draw needn't show every extreme that they name: `candidates`: each new video's 8 ids are distinct. The videos of id v are held by device v // 128. Of one device's pairs at most 2 name videos of one holder; in every draw some holders receive exactly 2 from every device.
All inputs are finite; a program needn't handle non-finite values.
Results may differ from a plain program's by a relative error of at most 0.0041.
Values may be sent and summed in bfloat16 or wider, within the bound.
A program may use at most 256 MiB of HBM per device.

v0:
```python
import math

import jax
import jax.numpy as jnp
from jax import lax
from jax.sharding import PartitionSpec as P

F = 8
R = 5
REGION_FEATURES = 1920


def conv_same(x, w):
    return lax.conv_general_dilated(
        x,
        w,
        (1, 1),
        "SAME",
        dimension_numbers=("NCHW", "OIHW", "NCHW"),
        preferred_element_type=jnp.float32,
    )


def pool_two(x):
    b, c, h, w = x.shape
    return jnp.max(x.reshape(b, c, h // 2, 2, w // 2, 2), axis=(3, 5))


def pair_scores(left, right, conv_one, conv_two, conv_three):
    count = left.shape[0]
    left_region_features = left.reshape(count, F * R, REGION_FEATURES)
    right_region_features = right.reshape(count, F * R, REGION_FEATURES)
    region_similarities = jnp.einsum(
        "avs,afs->avf",
        left_region_features,
        right_region_features,
        preferred_element_type=jnp.float32,
    ) * (1.0 / math.sqrt(REGION_FEATURES))
    region_similarities = region_similarities.reshape(count, F, R, F, R)
    frame_map = jnp.mean(jnp.max(region_similarities, axis=4), axis=2).astype(jnp.bfloat16)
    first = pool_two(jax.nn.relu(conv_same(frame_map[:, None], conv_one))).astype(jnp.bfloat16)
    second = pool_two(jax.nn.relu(conv_same(first, conv_two))).astype(jnp.bfloat16)
    final = conv_same(second, conv_three)[:, 0]
    return jnp.mean(jnp.max(jnp.clip(final, -1.0, 1.0), axis=2), axis=1)


def score_blocks(left_table, left_ids, right_table, right_ids, weights):
    count = left_ids.shape[0]
    block = math.gcd(count, 32)
    left_blocks = left_ids.reshape(count // block, block)
    right_blocks = right_ids.reshape(count // block, block)

    def one_block(pair_ids):
        return pair_scores(
            left_table[pair_ids[0]], right_table[pair_ids[1]], weights[0], weights[1], weights[2]
        )

    return lax.map(one_block, (left_blocks, right_blocks)).reshape(count)


def body(queries, index_videos, candidates, conv_one, conv_two, conv_three):
    devices = lax.axis_size("shard")
    q_dev = queries.shape[0]
    k_count = candidates.shape[1]
    idx_dev = index_videos.shape[0]
    frames = queries.shape[1]
    width = queries.shape[2]
    pairs = q_dev * k_count
    cap = max(2, (2 * pairs + devices - 1) // devices)
    weights = (conv_one, conv_two, conv_three)
    flat = candidates.reshape(pairs)
    holder = flat // idx_dev
    local = flat % idx_dev
    onehot = (holder[:, None] == jnp.arange(devices, dtype=jnp.int32)[None, :]).astype(jnp.int32)
    before = jnp.cumsum(onehot, axis=0) - onehot
    rank = jnp.sum(before * onehot, axis=1)
    slot = holder * cap + rank
    pair_query = jnp.arange(pairs) // k_count
    wanted = jnp.zeros((devices * cap,), jnp.int32).at[slot].set(local).reshape(devices, cap)
    rows = jnp.zeros((devices * cap, frames, width), jnp.bfloat16).at[slot].set(queries[pair_query])
    rows = rows.reshape(devices, cap, frames, width)
    got_rows = lax.all_to_all(rows, "shard", split_axis=0, concat_axis=0, tiled=True)
    received_ids = lax.all_to_all(wanted, "shard", split_axis=0, concat_axis=0, tiled=True)
    senders = got_rows.shape[0]
    items = got_rows.shape[1]
    table = got_rows.reshape(senders * items, frames, width)
    order = jnp.arange(senders * items, dtype=jnp.int32)
    result = score_blocks(
        table, order, index_videos, received_ids.reshape(senders * items), weights
    )
    scores_per_slot = result.reshape(senders, items)
    back = lax.all_to_all(scores_per_slot, "shard", split_axis=0, concat_axis=0, tiled=True)
    result = back.reshape(devices * cap)[slot]
    return result.reshape(q_dev, k_count)


def solution(mesh):
    placed = (P("shard", None, None), P("shard", None, None), P("shard", None), P(), P(), P())
    return jax.shard_map(
        body, mesh=mesh, in_specs=placed, out_specs=P("shard", None), check_vma=False
    )
```

profile of v0, /device:TPU:1, one launch (start us, length us, event | category | flops | bytes accessed | tf_op | source)
XLA Modules:
  0.0 1083.0 jit_solution(15504165776758101359)
XLA Ops:
  3.3 11.5 %all-to-all-start.1 = ((s32[128,1,2]{2,1,0:T(1,128)}), s32[128,1,2]{2,1,0:T(1,128)S(1)}, u32[]{:S(2)}, u32[]{:S(2)}) async-start(s32[128,1,2]{2,1,0:T(1,128)} %bitcast.13), calls=%async_computation.1 | async-start | bytes 131072 | tf_op jit(solution)/shard_map/all_to_all | solution.py:83
  14.9 9.5 gather_fusion.2
  24.3 13.0 %broadcast_in_dim.8 = bf16[256,8,9600]{2,1,0:T(8,128)(2,1)} broadcast(bf16[]{:T(256)} %constant.91.clone.1), dimensions={} | broadcast | bytes 39321600 | tf_op jit(solution)/shard_map/broadcast_in_dim | solution.py:80
  37.3 47.3 %scatter_fusion = bf16[256,8,9600]{2,1,0:T(8,128)(2,1)} fusion(bf16[256,8,9600]{2,1,0:T(8,128)(2,1)} %broadcast_in_dim.8, s32[128]{0:T(128)S(1)} %fusion.9, bf16[128,8,9600]{2,1,0:T(8,128)(2,1)} %gather_fusion.2), kind=kCustom, calls=%fused_computation.4 | custom fusion | bytes 58982912 | tf_op jit(solution)/shard_map/scatter | solution.py:80
  84.6 10.2 all-to-all-start
  96.4 552.2 %all-to-all-done = bf16[128,2,8,9600]{3,2,1,0:T(8,128)(2,1)} async-done(((bf16[128,2,8,9600]{3,2,1,0:T(8,128)(2,1)}), bf16[128,2,8,9600]{3,2,1,0:T(8,128)(2,1)}, u32[]{:S(2)}, u32[]{:S(2)}) %all-to-all-start) | async-done | bytes 39321632 | tf_op jit(solution)/shard_map/all_to_all | solution.py:82
  648.6 331.7 %while.10 = (s32[]{:T(128)}, f32[8,32]{1,0:T(8,128)S(1)}, bf16[1,64,3,3]{1,0,3,2:T(2,128)(2,1)S(1)}, s32[8,32]{1,0:T(8,128)S(1)}, bf16[256,8,9600]{2,1,0:T(8,128...) while((s32[]{:T(128)}, f32[8,32]{1,0:T(8,128)S(1)}, ...), condition=%wide.region_11.12_spmd, body=%wide.region_4.11_spmd.sunk | while | flops 211149248 | bytes 51030232 | solution.py:58
  654.3 9.0 reshape.361
  663.3 9.8 gather_fusion.1
  695.7 9.0 reshape.361
  704.8 9.8 gather_fusion.1
  737.2 9.0 reshape.361
  746.2 9.8 gather_fusion.1
  778.6 9.0 reshape.361
  787.7 9.8 gather_fusion.1
  829.1 9.8 gather_fusion.1
  861.6 9.0 reshape.361
  870.6 9.8 gather_fusion.1
  903.0 9.0 reshape.361
  912.1 9.8 gather_fusion.1
  944.5 9.0 reshape.361
  953.5 9.8 gather_fusion.1
  981.0 88.9 %all-to-all-start.2 = ((f32[128,1,2]{2,1,0:T(1,128)}), f32[128,1,2]{2,1,0:T(1,128)S(1)}, u32[]{:S(2)}, u32[]{:S(2)}) async-start(f32[128,1,2]{2,1,0:T(1,128)} %bitcast.14), calls=%async_computation.2 | async-start | bytes 131072 | tf_op jit(solution)/shard_map/all_to_all | solution.py:92
  1069.9 9.6 all-to-all-done.2
  (199 shorter events, 198.1 us)
Async XLA Ops:
  0.0 14.8 %copy-start = (bf16[16,8,9600]{2,1,0:T(8,128)(2,1)S(1)}, bf16[16,8,9600]{2,1,0:T(8,128)(2,1)}, u32[]{:S(2)}) copy-start(bf16[16,8,9600]{2,1,0:T(8,128)(2,1)} %param.8) | copy-start | bytes 7372804
  3.3 81.3 %all-to-all-start.1 = ((s32[128,1,2]{2,1,0:T(1,128)}), s32[128,1,2]{2,1,0:T(1,128)S(1)}, u32[]{:S(2)}, u32[]{:S(2)}) async-start(s32[128,1,2]{2,1,0:T(1,128)} %bitcast.13), calls=%async_computation.1 | async-start | bytes 131072 | tf_op jit(solution)/shard_map/all_to_all | solution.py:83
  84.6 10.2 copy-start.3
  84.6 10.2 copy-start.4
  84.6 564.0 %copy-start.2 = (bf16[64,32,3,3]{0,1,3,2:T(8,128)(2,1)S(1)}, bf16[64,32,3,3]{0,1,3,2:T(8,128)(2,1)}, u32[]{:S(2)}) copy-start(bf16[64,32,3,3]{0,1,3,2:T(8,128)(2,1)} %param.12) | copy-start | bytes 110596
  84.6 564.0 %all-to-all-start = ((bf16[128,2,8,9600]{3,2,1,0:T(8,128)(2,1)}), bf16[128,2,8,9600]{3,2,1,0:T(8,128)(2,1)}, u32[]{:S(2)}, u32[]{:S(2)}) async-start(bf16[128,2,8,9600]{3,2,1,0:T(8,128)(2,1)} %bitcast.61), calls=%async_computation | async-start | bytes 78643200 | tf_op jit(solution)/shard_map/all_to_all | solution.py:82
  980.3 102.7 %copy-start.1 = (bf16[16,8,9600]{2,1,0:T(8,128)(2,1)S(1)}, bf16[16,8,9600]{2,1,0:T(8,128)(2,1)}, u32[]{:S(2)}) copy-start(bf16[16,8,9600]{2,1,0:T(8,128)(2,1)} %param.8) | copy-start | bytes 7372804
  981.0 98.5 %all-to-all-start.2 = ((f32[128,1,2]{2,1,0:T(1,128)}), f32[128,1,2]{2,1,0:T(1,128)S(1)}, u32[]{:S(2)}, u32[]{:S(2)}) async-start(f32[128,1,2]{2,1,0:T(1,128)} %bitcast.14), calls=%async_computation.2 | async-start | bytes 131072 | tf_op jit(solution)/shard_map/all_to_all | solution.py:92
where the time goes:
time: 1090 us; the launch traced here: 1080 us
  waiting for transfers between devices  562 us (52%)
  local copies, waits for them, and re-layouts  348 us (32%)
  starting transfers between devices  111 us (10%)
  matrix products  53.9 us (5%)
    all_to_all x1, waiting for transfers between devices, body(): lax.all_to_all(rows, 'shard', split_axis=0, concat_axis=0, tiled=True)  552 us
    all_to_all x1, starting transfers between devices, body(): lax.all_to_all(scores_per_slot, 'shard', split_axis=0, concat_axis=0, til...  88.9 us
    gather x8, local copies, waits for them, and re-layouts, one_block(): right_table[pair_ids[1]]  78.4 us
    reshape x8, local copies, waits for them, and re-layouts, pair_scores(): left_region_features = left.reshape(count, F * R, REGION_FEATURES)  72.3 us
    reshape x8, local copies, waits for them, and re-layouts, pair_scores(): right_region_features = right.reshape(count, F * R, REGION_FEATURES)  72.1 us
    scatter x1, local copies, waits for them, and re-layouts, body(): jnp.zeros((devices * cap, frames, width), jnp.bfloat16).at[slot]  47.3 us
    gather x8, local copies, waits for them, and re-layouts, one_block(): left_table[pair_ids[0]]  45.1 us
    dot_general x8, matrix products, pair_scores(): jnp.einsum('avs,afs->avf', left_region_features, right_region_features, p...  43.2 us
  transfers between devices with their start and end apart: 3, of which 2 were waited for; matrix products, arithmetic and copies ran while one was open for 7% of the time, Pallas kernels for 0%

commit v1 on v0

v1 whole, which is shorter than its diff:
```python
import functools
import math

import jax
import jax.numpy as jnp
from jax import lax
from jax.experimental import pallas as pl
from jax.experimental.pallas import tpu as pltpu
from jax.sharding import PartitionSpec as P

MESH = pl.DeviceIdType.MESH
F = 8
R = 5
REGION_FEATURES = 1920
WIDTH = R * REGION_FEATURES
THIRD = WIDTH // 3
SIDE = 4
Q_DEV = 16
K = 8
DEVICES = 128
IDX_DEV = 128
SLOTS = 2 * DEVICES
AXES = ((0, 1, 2), (1, 2, 0), (2, 0, 1))


def position():
    i = lax.axis_index("shard")
    return (i // 32, (i // 8) % 4, (i // 2) % 4), i % 2


def device_at(chip, core):
    return ((chip[0] % 4) * 4 + chip[1] % 4) * 8 + (chip[2] % 4) * 2 + core % 2


def shifted(chip, axis, step):
    moved = list(chip)
    moved[axis] = moved[axis] + step
    return tuple(moved)


def greet(peers):
    barrier = pltpu.get_barrier_semaphore()
    for peer in peers:
        pl.semaphore_signal(barrier, inc=1, device_id=(peer,), device_id_type=MESH)
    pl.semaphore_wait(barrier, len(peers))


def gather_kernel(q_ref, g_ref, send_sem, recv_sem, local_sem):
    chip, core = position()
    near = {
        (axis, step): device_at(shifted(chip, axis, step), core) for axis in range(3) for step in (1, -1)
    }
    half = Q_DEV // 2
    greet(list(near.values()))
    started = []
    arrivals = {}

    span = {0: pl.ds(0, Q_DEV), 1: pl.ds(0, half), 2: pl.ds(half, half)}

    def send(t, axis_place, step, da, db, to_a, to_b, piece):
        number = len(started)
        axis = AXES[t][axis_place]
        if (da, db) == (0, 0):
            source = q_ref.at[span[piece], :, pl.ds(t * THIRD, THIRD)]
        else:
            source = g_ref.at[t, da, db, span[piece]]
        copy = pltpu.make_async_remote_copy(
            src_ref=source,
            dst_ref=g_ref.at[t, to_a, to_b, span[piece]],
            send_sem=send_sem.at[number],
            recv_sem=recv_sem.at[number],
            device_id=(near[axis, step],),
            device_id_type=MESH,
        )
        copy.start()
        started.append(copy)
        arrivals[t, to_a, to_b, piece] = copy

    def have(t, a, b, piece=0):
        arrivals[t, a, b, piece].wait_recv()

    def out_b(t, da):
        send(t, 1, 1, da, 0, da, 3, 0)
        send(t, 1, -1, da, 0, da, 1, 0)

    def on_b(t, da):
        have(t, da, 3)
        send(t, 1, 1, da, 3, da, 2, 1)
        have(t, da, 1)
        send(t, 1, -1, da, 1, da, 2, 2)

    thirds = range(3)
    for t in thirds:
        send(t, 0, 1, 0, 0, 3, 0, 0)
        send(t, 0, -1, 0, 0, 1, 0, 0)
    for t in thirds:
        out_b(t, 0)
    own = []
    for t in thirds:
        copy = pltpu.make_async_copy(
            q_ref.at[:, :, pl.ds(t * THIRD, THIRD)], g_ref.at[t, 0, 0], local_sem.at[t]
        )
        copy.start()
        own.append(copy)
    for t in thirds:
        have(t, 3, 0)
        send(t, 0, 1, 3, 0, 2, 0, 1)
        have(t, 1, 0)
        send(t, 0, -1, 1, 0, 2, 0, 2)
    for t in thirds:
        out_b(t, 3)
        out_b(t, 1)
    for t in thirds:
        on_b(t, 0)
    for t in thirds:
        have(t, 2, 0, 1)
        have(t, 2, 0, 2)
        out_b(t, 2)
    for da in (3, 1, 2):
        for t in thirds:
            on_b(t, da)
    for t in thirds:
        for da in range(4):
            have(t, da, 2, 1)
            have(t, da, 2, 2)
    for copy in started:
        copy.wait_send()
    for copy in own:
        copy.wait()


COPIES = 60
RING = 4


def exchange_kernel(
    sel_ref, g_ref, rows_ref, got_0, got_1, got_2, out, got_sem, send_sem, recv_sem
):
    got = (got_0, got_1, got_2)
    chip, core = position()
    peers = [device_at(chip, core + 1)]
    for axis in range(3):
        for step in (1, 2, 3):
            for other in (0, 1):
                peers.append(device_at(shifted(chip, axis, step), core + other))
    greet(peers)

    def fetch(block, t):
        return pltpu.make_async_copy(
            g_ref.at[t, block // 4, block % 4], got[t], got_sem.at[t]
        )

    def copies(block, t, slot):
        a, b, c = AXES[t]
        from_chip = shifted(shifted(chip, a, block // 4), b, block % 4)
        source = device_at(from_chip, core)
        made = []
        for step in range(4):
            for other in (0, 1):
                n = step * 2 + other
                src = out.at[slot, n]
                dst = rows_ref.at[source, :, :, pl.ds(t * THIRD, THIRD)]
                if n == 0:
                    made.append(pltpu.make_async_copy(src, dst, send_sem.at[slot, n]))
                else:
                    made.append(
                        pltpu.make_async_remote_copy(
                            src_ref=src,
                            dst_ref=dst,
                            send_sem=send_sem.at[slot, n],
                            recv_sem=recv_sem.at[t, block, n],
                            device_id=(device_at(shifted(chip, c, step), core + other),),
                            device_id_type=MESH,
                        )
                    )
        return made

    def drain(block, t, slot):
        for n, copy in enumerate(copies(block, t, slot)):
            if n == 0:
                copy.wait()
            else:
                copy.wait_send()

    for t in range(3):
        fetch(0, t).start()

    def one_block(block, carry):
        for t in range(3):
            slot = t * RING + block % RING

            @pl.when(block >= RING)
            def _():
                drain(block - RING, t, slot)

            fetch(block, t).wait()
            for n in range(8):
                for rank in range(2):
                    pick = sel_ref[((t * 16 + block) * 8 + n) * 2 + rank]
                    out[slot, n, rank] = got[t][pick]
            for copy in copies(block, t, slot):
                copy.start()

            @pl.when(block < 15)
            def _():
                fetch(block + 1, t).start()

        return carry

    lax.fori_loop(0, 16, one_block, 0)
    for t in range(3):
        for block in range(16 - RING, 16):
            drain(block, t, t * RING + block % RING)

    def settle(block, carry):
        for t in range(3):
            for copy in copies(block, t, 0)[1:]:
                copy.wait_recv()
        return carry

    lax.fori_loop(0, 16, settle, 0)


GROUP = 8


def frame_kernel(wanted_ref, rows_ref, videos_ref, map_ref):
    step = pl.program_id(0)

    def one_source(i, carry):
        for rank in range(2):
            want = wanted_ref[(step * GROUP + i) * 2 + rank]
            row = rows_ref[i, rank]
            video = videos_ref[want]
            left = jnp.concatenate(
                [row[:, r * REGION_FEATURES : (r + 1) * REGION_FEATURES] for r in range(R)], axis=0
            )
            right = jnp.concatenate(
                [video[:, r * REGION_FEATURES : (r + 1) * REGION_FEATURES] for r in range(R)], axis=0
            )
            sim = lax.dot_general(
                left, right, (((1,), (1,)), ((), ())), preferred_element_type=jnp.float32
            )
            best = sim[:, 0:F]
            for s in range(1, R):
                best = jnp.maximum(best, sim[:, s * F : (s + 1) * F])
            total = best[0:F]
            for r in range(1, R):
                total = total + best[r * F : (r + 1) * F]
            map_ref[i, rank] = total * (1.0 / (math.sqrt(REGION_FEATURES) * R))
        return carry

    lax.fori_loop(0, GROUP, one_source, 0)


def conv_same(x, w):
    return lax.conv_general_dilated(
        x, w, (1, 1), "SAME", dimension_numbers=("NCHW", "OIHW", "NCHW"), preferred_element_type=jnp.float32
    )


def pool_two(x):
    b, c, h, w = x.shape
    return jnp.max(x.reshape(b, c, h // 2, 2, w // 2, 2), axis=(3, 5))


def body(queries, index_videos, candidates, conv_one, conv_two, conv_three):
    chip, core = position()
    me = lax.axis_index("shard")
    pairs = Q_DEV * K

    gathered = pl.pallas_call(
        gather_kernel,
        out_shape=jax.ShapeDtypeStruct((3, SIDE, SIDE, Q_DEV, F, THIRD), jnp.bfloat16),
        in_specs=[pl.BlockSpec(memory_space=pl.ANY)],
        out_specs=pl.BlockSpec(memory_space=pl.ANY),
        scratch_shapes=[
            pltpu.SemaphoreType.DMA((COPIES,)),
            pltpu.SemaphoreType.DMA((COPIES,)),
            pltpu.SemaphoreType.DMA((3,)),
        ],
        compiler_params=pltpu.CompilerParams(collective_id=0, has_side_effects=True),
        name="gather",
    )(queries)

    flat = candidates.reshape(pairs)
    everyone = lax.all_gather(flat, "shard")
    holder = everyone // IDX_DEV
    local = everyone % IDX_DEV
    order = lax.broadcasted_iota(jnp.int32, (DEVICES, pairs), 1)
    mine = holder == me
    key = order * IDX_DEV + local
    low = jnp.min(jnp.where(mine, key, pairs * IDX_DEV), axis=1)
    high = jnp.max(jnp.where(mine, key, 0), axis=1)
    wanted = jnp.stack([low % IDX_DEV, high % IDX_DEV], axis=1).reshape(SLOTS)

    offset = jnp.arange(16, dtype=jnp.int32)
    sources, targets = [], []
    for a, b, c in AXES:
        sources.append(device_at(shifted(shifted(chip, a, offset // 4), b, offset % 4), core))
        line = jnp.arange(8, dtype=jnp.int32)
        targets.append(device_at(shifted(chip, c, line // 2), core + line % 2))
    sources = jnp.stack(sources)
    targets = jnp.stack(targets)
    asked = holder[sources]
    hit = asked[:, :, None, :] == targets[:, None, :, None]
    query_of = lax.broadcasted_iota(jnp.int32, (1, 1, 1, pairs), 3) // K
    first_pick = jnp.min(jnp.where(hit, query_of, Q_DEV - 1), axis=3)
    last_pick = jnp.max(jnp.where(hit, query_of, 0), axis=3)
    sel = jnp.stack([first_pick, last_pick], axis=3).reshape(3 * 16 * 8 * 2)

    rows = pl.pallas_call(
        exchange_kernel,
        out_shape=jax.ShapeDtypeStruct((DEVICES, 2, F, WIDTH), jnp.bfloat16),
        in_specs=[pl.BlockSpec(memory_space=pltpu.SMEM), pl.BlockSpec(memory_space=pl.ANY)],
        out_specs=pl.BlockSpec(memory_space=pl.ANY),
        scratch_shapes=[
            pltpu.VMEM((Q_DEV, F, THIRD), jnp.bfloat16),
            pltpu.VMEM((Q_DEV, F, THIRD), jnp.bfloat16),
            pltpu.VMEM((Q_DEV, F, THIRD), jnp.bfloat16),
            pltpu.VMEM((3 * RING, 8, 2, F, THIRD), jnp.bfloat16),
            pltpu.SemaphoreType.DMA((3,)),
            pltpu.SemaphoreType.DMA((3 * RING, 8)),
            pltpu.SemaphoreType.DMA((3, 16, 8)),
        ],
        compiler_params=pltpu.CompilerParams(
            collective_id=1, has_side_effects=True, vmem_limit_bytes=40 << 20
        ),
        name="exchange",
    )(sel, gathered)

    maps = pl.pallas_call(
        frame_kernel,
        out_shape=jax.ShapeDtypeStruct((DEVICES, 2, F, F), jnp.float32),
        grid_spec=pltpu.PrefetchScalarGridSpec(
            num_scalar_prefetch=1,
            grid=(DEVICES // GROUP,),
            in_specs=[
                pl.BlockSpec((GROUP, 2, F, WIDTH), lambda i, w: (i, 0, 0, 0)),
                pl.BlockSpec((IDX_DEV, F, WIDTH), lambda i, w: (0, 0, 0), pipeline_mode=pl.Buffered(1)),
            ],
            out_specs=pl.BlockSpec((GROUP, 2, F, F), lambda i, w: (i, 0, 0, 0)),
        ),
        compiler_params=pltpu.CompilerParams(vmem_limit_bytes=48 << 20),
        name="frames",
    )(wanted, rows, index_videos)

    frame_map = maps.reshape(SLOTS, 1, F, F).astype(jnp.bfloat16)
    first = pool_two(jax.nn.relu(conv_same(frame_map, conv_one))).astype(jnp.bfloat16)
    second = pool_two(jax.nn.relu(conv_same(first, conv_two))).astype(jnp.bfloat16)
    final = conv_same(second, conv_three)[:, 0]
    scores = jnp.mean(jnp.max(jnp.clip(final, -1.0, 1.0), axis=2), axis=1)

    back = lax.all_to_all(scores.reshape(DEVICES, 2), "shard", split_axis=0, concat_axis=0, tiled=True)
    my_holder = flat // IDX_DEV
    same = my_holder[:, None] == my_holder[None, :]
    earlier = jnp.arange(pairs)[None, :] < jnp.arange(pairs)[:, None]
    second_one = jnp.any(same & earlier, axis=1)
    to_me = my_holder[:, None] == jnp.arange(DEVICES)[None, :]
    score_first = jnp.sum(jnp.where(to_me, back[None, :, 0], 0.0), axis=1)
    score_last = jnp.sum(jnp.where(to_me, back[None, :, 1], 0.0), axis=1)
    return jnp.where(second_one, score_last, score_first).reshape(Q_DEV, K)


def solution(mesh):
    placed = (P("shard", None, None), P("shard", None, None), P("shard", None), P(), P(), P())
    return jax.shard_map(
        body, mesh=mesh, in_specs=placed, out_specs=P("shard", None), check_vma=False
    )
```

time: 1090 us -> 403 us (0.37)
  waiting for transfers between devices: 562 us -> 9.33 us
  Pallas kernels: 0 us -> 345 us
  local copies, waits for them, and re-layouts: 348 us -> 4.54 us
  starting transfers between devices: 111 us -> 5.41 us
  matrix products: 53.9 us -> 1.38 us
  blocking collectives: 0 us -> 34.4 us
    all_to_all x3 -> x1, waiting for transfers between devices: 562 us -> 9.33 us  [body(): lax.all_to_all(scores.reshape(DEVICES, 2), 'shard', split_axis=0, concat_...]
    pallas_call x0 -> x3, Pallas kernels: none -> 345 us  [the longest x1 154 us: body(): pl.pallas_call(exchange_kernel, out_shape=jax.ShapeDtypeStruct((DEVICES,...]
    reshape x27 -> x2, local copies, waits for them, and re-layouts: 146 us -> 0.28 us  [the longest x1 0.15 us: body(): sel = jnp.stack([first_pick, last_pick], axis=3).reshape(3 * 16 * 8 * 2)]
    gather x18 -> x1, local copies, waits for them, and re-layouts: 134 us -> 0.59 us  [body(): asked = holder[sources]]
    all_to_all x3 -> x1, starting transfers between devices: 111 us -> 5.41 us  [body(): lax.all_to_all(scores.reshape(DEVICES, 2), 'shard', split_axis=0, concat_...]
    scatter x2 -> x0, local copies, waits for them, and re-layouts: 48.3 us -> none  [the longest x1 47.3 us: body(): jnp.zeros((devices * cap, frames, width), jnp.bfloat16).at[slot]]
    dot_general x8 -> x0, matrix products: 43.2 us -> none  [pair_scores(): jnp.einsum('avs,afs->avf', left_region_features, right_region_features, p...]
    all_gather x0 -> x1, blocking collectives: none -> 34.4 us  [body(): everyone = lax.all_gather(flat, 'shard')]
  transfers between devices with their start and end apart: 3 -> 1, of which waited for: 2 -> 1; matrix products, arithmetic and copies ran while one was open for 7% -> 0% of each run, Pallas kernels for 0% -> 0%
where the time goes in v1:
time: 403 us
  Pallas kernels  345 us (86%)
  blocking collectives  34.4 us (9%)
  waiting for transfers between devices  9.33 us (2%)
  starting transfers between devices  5.41 us (1%)
  local copies, waits for them, and re-layouts  4.54 us (1%)
    pallas_call x1, Pallas kernels, body(): pl.pallas_call(exchange_kernel, out_shape=jax.ShapeDtypeStruct((DEVICES,...  154 us
    pallas_call x1, Pallas kernels, body(): pl.pallas_call(gather_kernel, out_shape=jax.ShapeDtypeStruct((3, SIDE, SI...  137 us
    pallas_call x1, Pallas kernels, body(): pl.pallas_call(frame_kernel, out_shape=jax.ShapeDtypeStruct((DEVICES, 2,...  53.9 us
    all_gather x1, blocking collectives, body(): everyone = lax.all_gather(flat, 'shard')  34.4 us
    all_to_all x1, waiting for transfers between devices, body(): lax.all_to_all(scores.reshape(DEVICES, 2), 'shard', split_axis=0, concat_...  9.33 us
  transfers between devices with their start and end apart: 1, of which 1 were waited for; matrix products, arithmetic and copies ran while one was open for 0% of the time, Pallas kernels for 0%

profile of v1, /device:TPU:1, one launch (start us, length us, event | category | flops | bytes accessed | tf_op | source)
XLA Modules:
  0.0 402.8 jit_solution(16394435381105556502)
XLA Ops:
  0.2 0.8 copy.40
  1.1 34.4 %all-gather = s32[128,1,128]{2,1,0:T(1,128)S(1)} all-gather(s32[1,1,128]{2,1,0:T(1,128)S(1)} %reshape.862), channel_id=1, replica_groups=mesh['shard'=128] {'shard'}, dimensions={0}, use_global_device_ids=true | all-gather | bytes 66048 | tf_op jit(solution)/shard_map/all_gather | solution.py:287
  35.6 0.1 select_reduce_fusion.3
  35.7 0.1 copy.42
  35.8 0.1 reshape.849.wanted_ref
  36.1 0.6 gather_fusion
  36.7 1.8 fusion.2
  38.6 0.2 copy.45
  38.9 0.1 reshape.850.sel_ref
  39.0 136.7 %gather.7.g_ref = bf16[3,4,4,16,8,3200]{5,4,3,2,1,0:T(8,128)(2,1)} custom-call(bf16[16,8,9600]{2,1,0:T(8,128)(2,1)} %q_ref.1), custom_call_target="tpu_custom_call" | custom-call | tf_op jit(solution)/shard_map/gather/pallas_call | solution.py:272
  175.7 153.9 %exchange.1.rows_ref = bf16[128,2,8,9600]{3,2,1,0:T(8,128)(2,1)} custom-call(s32[768]{0:T(1024)S(1)} %reshape.850.sel_ref, bf16[3,4,4,16,8,3200]{5,4,3,2,1,0:T(8,128)(2,1)} %gather.7.g_ref), custom_call_target="tpu_custom_call" | custom-call | tf_op jit(solution)/shard_map/exchange/pallas_call | solution.py:312
  329.7 53.9 %frames.1 = f32[128,2,8,8]{3,2,1,0:T(8,128)S(1)} custom-call(s32[256]{0:T(256)S(1)} %reshape.849.wanted_ref, bf16[128,2,8,9600]{3,2,1,0:T(8,128)(2,1)} %exchange.1.rows_ref, bf16[128,8,9600]{2,1,0:T(8,128)(2,1)} %videos_ref.1), custom_call_target="tpu_custom_call" | custom-call | tf_op jit(solution)/shard_map/frames/pallas_call | solution.py:332
  383.7 0.4 copy.46
  384.1 0.5 convolution_maximum_fusion
  384.7 0.2 reduce_max.50
  384.9 0.6 convolution_maximum_fusion.1
  385.6 0.2 fusion
  385.9 0.8 div.118
  386.6 5.4 %all-to-all-start = ((f32[128,1,2]{2,1,0:T(1,128)}), f32[128,1,2]{2,1,0:T(1,128)S(1)}, u32[]{:S(2)}, u32[]{:S(2)}) async-start(f32[128,1,2]{2,1,0:T(1,128)} %bitcast.12), calls=%async_computation | async-start | bytes 131072 | tf_op jit(solution)/shard_map/all_to_all | solution.py:354
  392.2 0.2 fusion.7
  392.3 9.3 %all-to-all-done = f32[128,1,2]{2,1,0:T(1,128)S(1)} async-done(((f32[128,1,2]{2,1,0:T(1,128)}), f32[128,1,2]{2,1,0:T(1,128)S(1)}, u32[]{:S(2)}, u32[]{:S(2)}) %all-to-all-start) | async-done | bytes 1056 | tf_op jit(solution)/shard_map/all_to_all | solution.py:354
  401.7 0.2 slice_reduce_fusion
  401.8 0.2 select_reduce_fusion
  402.1 0.7 copy.50
  (32 shorter events, 0.9 us)
Async XLA Ops:
  0.0 384.9 %copy-start = (bf16[64,32,3,3]{0,1,3,2:T(8,128)(2,1)S(1)}, bf16[64,32,3,3]{0,1,3,2:T(8,128)(2,1)}, u32[]{:S(2)}) copy-start(bf16[64,32,3,3]{0,1,3,2:T(8,128)(2,1)} %param.10) | copy-start | bytes 110596
  329.7 54.4 %copy-start.1 = (bf16[32,1,3,3]{0,3,2,1:T(4,128)(2,1)S(1)}, bf16[32,1,3,3]{0,3,2,1:T(4,128)(2,1)}, u32[]{:S(2)}) copy-start(bf16[32,1,3,3]{0,3,2,1:T(4,128)(2,1)} %param.9) | copy-start | bytes 1732
  383.6 1.9 copy-start.2
  386.6 15.0 %all-to-all-start = ((f32[128,1,2]{2,1,0:T(1,128)}), f32[128,1,2]{2,1,0:T(1,128)S(1)}, u32[]{:S(2)}, u32[]{:S(2)}) async-start(f32[128,1,2]{2,1,0:T(1,128)} %bitcast.12), calls=%async_computation | async-start | bytes 131072 | tf_op jit(solution)/shard_map/all_to_all | solution.py:354

commit v2 on v1

v2 whole, which is shorter than its diff:
```python
import functools
import math

import jax
import jax.numpy as jnp
from jax import lax
from jax.experimental import pallas as pl
from jax.experimental.pallas import tpu as pltpu
from jax.sharding import PartitionSpec as P

MESH = pl.DeviceIdType.MESH
F = 8
R = 5
REGION_FEATURES = 1920
WIDTH = R * REGION_FEATURES
THIRD = WIDTH // 3
PART = REGION_FEATURES // 3
SIDE = 4
Q_DEV = 16
K = 8
DEVICES = 128
IDX_DEV = 128
SLOTS = 2 * DEVICES
AXES = ((0, 1, 2), (1, 2, 0), (2, 0, 1))


def position():
    i = lax.axis_index("shard")
    return (i // 32, (i // 8) % 4, (i // 2) % 4), i % 2


def device_at(chip, core):
    return ((chip[0] % 4) * 4 + chip[1] % 4) * 8 + (chip[2] % 4) * 2 + core % 2


def shifted(chip, axis, step):
    moved = list(chip)
    moved[axis] = moved[axis] + step
    return tuple(moved)


def greet(peers):
    barrier = pltpu.get_barrier_semaphore()
    for peer in peers:
        pl.semaphore_signal(barrier, inc=1, device_id=(peer,), device_id_type=MESH)
    pl.semaphore_wait(barrier, len(peers))


def gather_kernel(q_ref, ids_ref, g_ref, table_ref, send_sem, recv_sem, local_sem, id_send, id_recv):
    chip, core = position()
    near = {
        (axis, step): device_at(shifted(chip, axis, step), core) for axis in range(3) for step in (1, 2, 3)
    }
    sibling = device_at(chip, core + 1)
    half = Q_DEV // 2
    own = []
    for t in range(3):
        for r in range(R):
            copy = pltpu.make_async_copy(
                q_ref.at[:, :, pl.ds(r * REGION_FEATURES + t * PART, PART)],
                g_ref.at[t, 0, 0, :, :, pl.ds(r * PART, PART)],
                local_sem.at[t, r],
            )
            own.append(copy)
    me = device_at(chip, core)
    own_ids = pltpu.make_async_copy(ids_ref, table_ref.at[pl.ds(me, 1)], local_sem.at[3, 0])
    own_ids.start()
    greet(list(near.values()) + [sibling])
    started = []
    arrivals = {}

    span = {0: pl.ds(0, Q_DEV), 1: pl.ds(0, half), 2: pl.ds(half, half)}

    def send_own(t, axis_place, step, to_a, to_b):
        axis = AXES[t][axis_place]
        for r in range(R):
            number = len(started)
            copy = pltpu.make_async_remote_copy(
                src_ref=q_ref.at[:, :, pl.ds(r * REGION_FEATURES + t * PART, PART)],
                dst_ref=g_ref.at[t, to_a, to_b, :, :, pl.ds(r * PART, PART)],
                send_sem=send_sem.at[number],
                recv_sem=recv_sem.at[number],
                device_id=(near[axis, step],),
                device_id_type=MESH,
            )
            copy.start()
            started.append(copy)
            arrivals[t, to_a, to_b, 3 + r] = copy

    def send(t, axis_place, step, da, db, to_a, to_b, piece):
        number = len(started)
        axis = AXES[t][axis_place]
        copy = pltpu.make_async_remote_copy(
            src_ref=g_ref.at[t, da, db, span[piece]],
            dst_ref=g_ref.at[t, to_a, to_b, span[piece]],
            send_sem=send_sem.at[number],
            recv_sem=recv_sem.at[number],
            device_id=(near[axis, step],),
            device_id_type=MESH,
        )
        copy.start()
        started.append(copy)
        arrivals[t, to_a, to_b, piece] = copy

    def have(t, a, b, piece=0):
        if (t, a, b, piece) in arrivals:
            arrivals[t, a, b, piece].wait_recv()
        else:
            for r in range(R):
                arrivals[t, a, b, 3 + r].wait_recv()

    def out_b(t, da):
        if da == 0:
            send_own(t, 1, 1, 0, 3)
            send_own(t, 1, 3, 0, 1)
        else:
            send(t, 1, 1, da, 0, da, 3, 0)
            send(t, 1, 3, da, 0, da, 1, 0)

    def on_b(t, da):
        have(t, da, 3)
        send(t, 1, 1, da, 3, da, 2, 1)
        have(t, da, 1)
        send(t, 1, 3, da, 1, da, 2, 2)

    id_copies = []

    def send_ids(first, count, peers):
        made = []
        for peer in peers:
            number = len(id_copies)
            copy = pltpu.make_async_remote_copy(
                src_ref=table_ref.at[pl.ds(first, count)],
                dst_ref=table_ref.at[pl.ds(first, count)],
                send_sem=id_send.at[number],
                recv_sem=id_recv.at[number],
                device_id=(peer,),
                device_id_type=MESH,
            )
            copy.start()
            made.append(copy)
            id_copies.append(copy)
        return made

    def line(axis):
        return [near[axis, step] for step in (1, 2, 3)]

    thirds = range(3)
    own_ids.wait()
    wave = send_ids(me, 1, [sibling])
    for t in thirds:
        send_own(t, 0, 1, 3, 0)
        send_own(t, 0, 3, 1, 0)
    for copy in wave:
        copy.wait_recv()
    wave = send_ids(me - core, 2, line(2))
    for t in thirds:
        out_b(t, 0)
    for copy in own:
        copy.start()
    for t in thirds:
        have(t, 3, 0)
        send(t, 0, 1, 3, 0, 2, 0, 1)
        have(t, 1, 0)
        send(t, 0, 3, 1, 0, 2, 0, 2)
    for t in thirds:
        out_b(t, 3)
        out_b(t, 1)
    for t in thirds:
        on_b(t, 0)
    for copy in wave:
        copy.wait_recv()
    wave = send_ids((me // 8) * 8, 8, line(1))
    for t in thirds:
        have(t, 2, 0, 1)
        have(t, 2, 0, 2)
        out_b(t, 2)
    for t in thirds:
        on_b(t, 3)
    for copy in wave:
        copy.wait_recv()
    wave = send_ids((me // 32) * 32, 32, line(0))
    for da in (1, 2):
        for t in thirds:
            on_b(t, da)
    for t in thirds:
        for da in range(4):
            have(t, da, 2, 1)
            have(t, da, 2, 2)
    for copy in wave:
        copy.wait_recv()
    for copy in started + id_copies:
        copy.wait_send()
    for copy in own:
        copy.wait()


COPIES = 108
RING = 4
LAG = 3
BLOCKS = SIDE * SIDE


def score_kernel(
    sel_ref, wanted_ref, g_ref, videos_ref, rows_ref, map_ref,
    got_0, got_1, got_2, out, row, videos, sims,
    got_sem, send_sem, recv_sem, self_sem, row_sem, video_sem,
):
    got = (got_0, got_1, got_2)
    chip, core = position()
    load_videos = pltpu.make_async_copy(videos_ref, videos, video_sem)
    load_videos.start()
    peers = [device_at(chip, core + 1)]
    for axis in range(3):
        for step in (1, 2, 3):
            for other in (0, 1):
                peers.append(device_at(shifted(chip, axis, step), core + other))
    greet(peers)

    def fetch(block, t):
        return pltpu.make_async_copy(
            g_ref.at[t, block // 4, block % 4], got[t], got_sem.at[t]
        )

    def copies(block, t):
        slot = t * RING + block % RING
        made = []
        for step in range(4):
            for other in (0, 1):
                n = step * 2 + other
                if n > 0:
                    made.append(
                        pltpu.make_async_remote_copy(
                            src_ref=out.at[slot, n],
                            dst_ref=rows_ref.at[t, block, n],
                            send_sem=send_sem.at[slot, n],
                            recv_sem=recv_sem.at[t, block, n],
                            device_id=(device_at(shifted(chip, AXES[t][2], step), core + other),),
                            device_id_type=MESH,
                        )
                    )
        return made

    def keep(block, t):
        slot = t * RING + block % RING
        return pltpu.make_async_copy(out.at[slot, 0], rows_ref.at[t, block, 0], self_sem.at[slot])

    def load_row(block, t):
        return pltpu.make_async_copy(rows_ref.at[t, block], row.at[t], row_sem.at[t])

    def drain(block, t):
        for copy in copies(block, t):
            copy.wait_send()

    for t in range(3):
        fetch(0, t).start()

    def pack(block, t):
        @pl.when(block >= RING)
        def _():
            drain(block - RING, t)

        fetch(block, t).wait()
        slot = t * RING + block % RING
        for n in range(8):
            for rank in range(2):
                pick = sel_ref[((t * BLOCKS + block) * 8 + n) * 2 + rank]
                out[slot, n, rank] = got[t][pick]
        for copy in copies(block, t):
            copy.start()
        keep(block, t).start()

        @pl.when(block < BLOCKS - 1)
        def _():
            fetch(block + 1, t).start()

    def receive(block, t):
        for copy in copies(block, t):
            copy.wait_recv()
        keep(block, t).wait()
        load_row(block, t).start()

    def add_up(block, t):
        load_row(block, t).wait()
        a, b, c = AXES[t]
        from_line = shifted(shifted(chip, a, block // 4), b, block % 4)

        def one(n, carry):
            source = device_at(shifted(from_line, c, 4 - n // 2), core + n % 2)
            for rank in range(2):
                at = source * 2 + rank
                want = wanted_ref[at]
                left = jnp.concatenate(
                    [row[t, n, rank, :, r * PART : (r + 1) * PART] for r in range(R)], axis=0
                )
                right = jnp.concatenate(
                    [
                        videos[want, :, pl.ds(s * REGION_FEATURES + t * PART, PART)]
                        for s in range(R)
                    ],
                    axis=0,
                )
                sims[at] += lax.dot_general(
                    left, right, (((1,), (1,)), ((), ())), preferred_element_type=jnp.float32
                )
            return carry

        lax.fori_loop(0, 8, one, 0)

    def one_block(block, carry):
        @pl.when(block == LAG)
        def _():
            sims[...] = jnp.zeros_like(sims)
            load_videos.wait()

        for t in range(3):
            @pl.when(block < BLOCKS)
            def _():
                pack(block, t)

            @pl.when(jnp.logical_and(block > LAG, block <= BLOCKS + LAG))
            def _():
                add_up(block - LAG - 1, t)

            @pl.when(jnp.logical_and(block >= LAG, block < BLOCKS + LAG))
            def _():
                receive(block - LAG, t)

        return carry

    lax.fori_loop(0, BLOCKS + LAG + 1, one_block, 0)
    for t in range(3):
        for block in range(BLOCKS - RING, BLOCKS):
            drain(block, t)

    def finish(at, carry):
        sim = sims[at]
        best = sim[:, 0:F]
        for s in range(1, R):
            best = jnp.maximum(best, sim[:, s * F : (s + 1) * F])
        total = best[0:F]
        for r in range(1, R):
            total = total + best[r * F : (r + 1) * F]
        map_ref[at] = total * (1.0 / (math.sqrt(REGION_FEATURES) * R))
        return carry

    lax.fori_loop(0, SLOTS, finish, 0, unroll=4)


def conv_same(x, w):
    return lax.conv_general_dilated(
        x, w, (1, 1), "SAME", dimension_numbers=("NCHW", "OIHW", "NCHW"), preferred_element_type=jnp.float32
    )


def pool_two(x):
    b, c, h, w = x.shape
    return jnp.max(x.reshape(b, c, h // 2, 2, w // 2, 2), axis=(3, 5))


def body(queries, index_videos, candidates, conv_one, conv_two, conv_three):
    chip, core = position()
    me = lax.axis_index("shard")
    pairs = Q_DEV * K

    flat = candidates.reshape(pairs)
    gathered, everyone = pl.pallas_call(
        gather_kernel,
        out_shape=(
            jax.ShapeDtypeStruct((3, SIDE, SIDE, Q_DEV, F, THIRD), jnp.bfloat16),
            jax.ShapeDtypeStruct((DEVICES, 1, pairs), jnp.int32),
        ),
        in_specs=[pl.BlockSpec(memory_space=pl.ANY)] * 2,
        out_specs=(pl.BlockSpec(memory_space=pl.ANY), pl.BlockSpec(memory_space=pl.ANY)),
        scratch_shapes=[
            pltpu.SemaphoreType.DMA((COPIES,)),
            pltpu.SemaphoreType.DMA((COPIES,)),
            pltpu.SemaphoreType.DMA((4, R)),
            pltpu.SemaphoreType.DMA((10,)),
            pltpu.SemaphoreType.DMA((10,)),
        ],
        compiler_params=pltpu.CompilerParams(collective_id=0, has_side_effects=True),
        name="gather",
    )(queries, flat.reshape(1, 1, pairs))
    everyone = everyone.reshape(DEVICES, pairs)
    holder = everyone // IDX_DEV
    local = everyone % IDX_DEV
    order = lax.broadcasted_iota(jnp.int32, (DEVICES, pairs), 1)
    mine = holder == me
    key = order * IDX_DEV + local
    low = jnp.min(jnp.where(mine, key, pairs * IDX_DEV), axis=1)
    high = jnp.max(jnp.where(mine, key, 0), axis=1)
    wanted = jnp.stack([low % IDX_DEV, high % IDX_DEV], axis=1).reshape(SLOTS)

    offset = jnp.arange(16, dtype=jnp.int32)
    sources, targets = [], []
    for a, b, c in AXES:
        sources.append(device_at(shifted(shifted(chip, a, offset // 4), b, offset % 4), core))
        line = jnp.arange(8, dtype=jnp.int32)
        targets.append(device_at(shifted(chip, c, line // 2), core + line % 2))
    sources = jnp.stack(sources)
    targets = jnp.stack(targets)
    asked = holder[sources]
    hit = asked[:, :, None, :] == targets[:, None, :, None]
    query_of = lax.broadcasted_iota(jnp.int32, (1, 1, 1, pairs), 3) // K
    first_pick = jnp.min(jnp.where(hit, query_of, Q_DEV - 1), axis=3)
    last_pick = jnp.max(jnp.where(hit, query_of, 0), axis=3)
    sel = jnp.stack([first_pick, last_pick], axis=3).reshape(3 * 16 * 8 * 2)

    _, maps = pl.pallas_call(
        score_kernel,
        out_shape=(
            jax.ShapeDtypeStruct((3, BLOCKS, 8, 2, F, THIRD), jnp.bfloat16),
            jax.ShapeDtypeStruct((SLOTS, F, F), jnp.float32),
        ),
        in_specs=[
            pl.BlockSpec(memory_space=pltpu.SMEM),
            pl.BlockSpec(memory_space=pltpu.SMEM),
            pl.BlockSpec(memory_space=pl.ANY),
            pl.BlockSpec(memory_space=pl.ANY),
        ],
        out_specs=(
            pl.BlockSpec(memory_space=pl.ANY),
            pl.BlockSpec(memory_space=pltpu.VMEM),
        ),
        scratch_shapes=[
            pltpu.VMEM((Q_DEV, F, THIRD), jnp.bfloat16),
            pltpu.VMEM((Q_DEV, F, THIRD), jnp.bfloat16),
            pltpu.VMEM((Q_DEV, F, THIRD), jnp.bfloat16),
            pltpu.VMEM((3 * RING, 8, 2, F, THIRD), jnp.bfloat16),
            pltpu.VMEM((3, 8, 2, F, THIRD), jnp.bfloat16),
            pltpu.VMEM((IDX_DEV, F, WIDTH), jnp.bfloat16),
            pltpu.VMEM((SLOTS, F * R, F * R), jnp.float32),
            pltpu.SemaphoreType.DMA((3,)),
            pltpu.SemaphoreType.DMA((3 * RING, 8)),
            pltpu.SemaphoreType.DMA((3, BLOCKS, 8)),
            pltpu.SemaphoreType.DMA((3 * RING,)),
            pltpu.SemaphoreType.DMA((3,)),
            pltpu.SemaphoreType.DMA,
        ],
        compiler_params=pltpu.CompilerParams(
            collective_id=1, has_side_effects=True, vmem_limit_bytes=56 << 20
        ),
        name="score",
    )(sel, wanted, gathered, index_videos)

    frame_map = maps.reshape(SLOTS, 1, F, F).astype(jnp.bfloat16)
    first = pool_two(jax.nn.relu(conv_same(frame_map, conv_one))).astype(jnp.bfloat16)
    second = pool_two(jax.nn.relu(conv_same(first, conv_two))).astype(jnp.bfloat16)
    final = conv_same(second, conv_three)[:, 0]
    scores = jnp.mean(jnp.max(jnp.clip(final, -1.0, 1.0), axis=2), axis=1)

    back = lax.all_to_all(scores.reshape(DEVICES, 2), "shard", split_axis=0, concat_axis=0, tiled=True)
    my_holder = flat // IDX_DEV
    same = my_holder[:, None] == my_holder[None, :]
    earlier = jnp.arange(pairs)[None, :] < jnp.arange(pairs)[:, None]
    second_one = jnp.any(same & earlier, axis=1)
    to_me = my_holder[:, None] == jnp.arange(DEVICES)[None, :]
    score_first = jnp.sum(jnp.where(to_me, back[None, :, 0], 0.0), axis=1)
    score_last = jnp.sum(jnp.where(to_me, back[None, :, 1], 0.0), axis=1)
    return jnp.where(second_one, score_last, score_first).reshape(Q_DEV, K)


def solution(mesh):
    placed = (P("shard", None, None), P("shard", None, None), P("shard", None), P(), P(), P())
    return jax.shard_map(
        body, mesh=mesh, in_specs=placed, out_specs=P("shard", None), check_vma=False
    )
```

time: 403 us -> 347 us (0.86)
  blocking collectives: 34.4 us -> 0 us
  Pallas kernels: 345 us -> 318 us
    all_gather x1 -> x0, blocking collectives: 34.4 us -> none  [body(): everyone = lax.all_gather(flat, 'shard')]
    pallas_call x3 -> x2, Pallas kernels: 345 us -> 318 us  [the longest x1 176 us: body(): pl.pallas_call(score_kernel, out_shape=(jax.ShapeDtypeStruct((3, BLOCKS,...]
where the time goes in v2:
time: 347 us; the launch traced here: 346 us
  Pallas kernels  318 us (92%)
  waiting for transfers between devices  9.33 us (3%)
  local copies, waits for them, and re-layouts  6.24 us (2%)
  other arithmetic  5.72 us (2%)
  starting transfers between devices  5 us (1%)
    pallas_call x1, Pallas kernels, body(): pl.pallas_call(score_kernel, out_shape=(jax.ShapeDtypeStruct((3, BLOCKS,...  176 us
    pallas_call x1, Pallas kernels, body(): pl.pallas_call(gather_kernel, out_shape=(jax.ShapeDtypeStruct((3, SIDE, S...  143 us
    all_to_all x1, waiting for transfers between devices, body(): lax.all_to_all(scores.reshape(DEVICES, 2), 'shard', split_axis=0, concat_...  9.33 us
  transfers between devices with their start and end apart: 1, of which 1 were waited for; matrix products, arithmetic and copies ran while one was open for 0% of the time, Pallas kernels for 0%

profile of v2, /device:TPU:1, one launch (start us, length us, event | category | flops | bytes accessed | tf_op | source)
XLA Modules:
  0.0 346.1 jit_solution(2142930369279220560)
XLA Ops:
  0.1 0.8 copy.37
  0.9 0.6 reshape_reshape.3.ids_ref
  1.5 142.8 %gather.7 = (bf16[3,4,4,16,8,3200]{5,4,3,2,1,0:T(8,128)(2,1)}, s32[128,1,128]{2,1,0:T(1,128)}) custom-call(bf16[16,8,9600]{2,1,0:T(8,128)(2,1)} %q_ref.1, s32[1,1,128]{2,1,0:T(1,128)} %reshape_reshape.3.ids_ref), custom_call_target="tpu_custom_call" | custom-call | tf_op jit(solution)/shard_map/gather/pallas_call | solution.py:367
  144.3 0.9 broadcast_compare_fusion
  145.3 0.6 gather_fusion
  145.9 1.8 fusion.2
  147.8 0.2 copy.41
  148.0 0.7 reshape.838.sel_ref
  148.8 1.0 select_reduce_fusion.3
  149.9 0.7 reshape.839.wanted_ref
  150.6 175.5 %score.1 = (bf16[3,16,8,2,8,3200]{5,4,3,2,1,0:T(8,128)(2,1)}, f32[256,8,8]{2,1,0:T(8,128)}) custom-call(s32[768]{0:T(1024)} %reshape.838.sel_ref, s32[256]{0:T(256)} %reshape.839.wanted_ref, bf16[3,4,4,16,8,3200]{5,4,3,2,1,0:T(8,128)(2,1)} %get-tuple-element.9.g_ref, bf16[128,8,9600]{2,1,0:T(8,128)(2,1)} %videos_ref.1), custom_call_target="tpu_custom_call" | custom-call | tf_op jit(solution)/shard_map/score/pallas_call | solution.py:410
  326.1 1.3 convert_bitcast_fusion
  327.4 0.4 copy.43
  327.9 0.5 convolution_maximum_fusion
  328.4 0.2 reduce_max.50
  328.6 0.6 convolution_maximum_fusion.1
  329.4 0.2 fusion
  329.6 0.8 div.118
  330.4 5.0 %all-to-all-start = ((f32[128,1,2]{2,1,0:T(1,128)}), f32[128,1,2]{2,1,0:T(1,128)S(1)}, u32[]{:S(2)}, u32[]{:S(2)}) async-start(f32[128,1,2]{2,1,0:T(1,128)} %bitcast.12), calls=%async_computation | async-start | bytes 131072 | tf_op jit(solution)/shard_map/all_to_all | solution.py:453
  335.5 0.2 fusion.7
  335.7 9.3 %all-to-all-done = f32[128,1,2]{2,1,0:T(1,128)S(1)} async-done(((f32[128,1,2]{2,1,0:T(1,128)}), f32[128,1,2]{2,1,0:T(1,128)S(1)}, u32[]{:S(2)}, u32[]{:S(2)}) %all-to-all-start) | async-done | bytes 1056 | tf_op jit(solution)/shard_map/all_to_all | solution.py:453
  345.0 0.2 slice_reduce_fusion
  345.2 0.2 select_reduce_fusion
  345.5 0.7 copy.47
  (30 shorter events, 0.8 us)
Async XLA Ops:
  0.0 328.6 %copy-start = (bf16[64,32,3,3]{0,1,3,2:T(8,128)(2,1)S(1)}, bf16[64,32,3,3]{0,1,3,2:T(8,128)(2,1)}, u32[]{:S(2)}) copy-start(bf16[64,32,3,3]{0,1,3,2:T(8,128)(2,1)} %param.10) | copy-start | bytes 110596
  150.6 177.2 %copy-start.1 = (bf16[32,1,3,3]{0,3,2,1:T(4,128)(2,1)S(1)}, bf16[32,1,3,3]{0,3,2,1:T(4,128)(2,1)}, u32[]{:S(2)}) copy-start(bf16[32,1,3,3]{0,3,2,1:T(4,128)(2,1)} %param.9) | copy-start | bytes 1732
  327.4 1.9 copy-start.2
  330.4 14.6 %all-to-all-start = ((f32[128,1,2]{2,1,0:T(1,128)}), f32[128,1,2]{2,1,0:T(1,128)S(1)}, u32[]{:S(2)}, u32[]{:S(2)}) async-start(f32[128,1,2]{2,1,0:T(1,128)} %bitcast.12), calls=%async_computation | async-start | bytes 131072 | tf_op jit(solution)/shard_map/all_to_all | solution.py:453

commit v3 on v2

--- a/solution.py
+++ b/solution.py
@@ -46,8 +46,7 @@
     pl.semaphore_wait(barrier, len(peers))
 
 
-def gather_kernel(q_ref, ids_ref, g_ref, table_ref, send_sem, recv_sem, local_sem, id_send, id_recv):
-    chip, core = position()
+def gather(chip, core, q_ref, ids_ref, g_ref, table_ref, make_tables, send_sem, recv_sem, local_sem, id_send, id_recv):
     near = {
         (axis, step): device_at(shifted(chip, axis, step), core) for axis in range(3) for step in (1, 2, 3)
     }
@@ -65,7 +64,6 @@
     me = device_at(chip, core)
     own_ids = pltpu.make_async_copy(ids_ref, table_ref.at[pl.ds(me, 1)], local_sem.at[3, 0])
     own_ids.start()
-    greet(list(near.values()) + [sibling])
     started = []
     arrivals = {}
 
@@ -180,19 +178,27 @@
     for copy in wave:
         copy.wait_recv()
     wave = send_ids((me // 32) * 32, 32, line(0))
-    for da in (1, 2):
-        for t in thirds:
-            on_b(t, da)
-    for t in thirds:
-        for da in range(4):
-            have(t, da, 2, 1)
-            have(t, da, 2, 2)
+    for t in thirds:
+        on_b(t, 1)
     for copy in wave:
         copy.wait_recv()
-    for copy in started + id_copies:
-        copy.wait_send()
+    make_tables()
+    for t in thirds:
+        on_b(t, 2)
     for copy in own:
         copy.wait()
+
+    def the_rest():
+        for t in thirds:
+            for da in range(4):
+                have(t, da, 2, 1)
+                have(t, da, 2, 2)
+
+    def all_sent():
+        for copy in started + id_copies:
+            copy.wait_send()
+
+    return the_rest, all_sent
 
 
 COPIES = 108
@@ -201,26 +207,83 @@
 BLOCKS = SIDE * SIDE
 
 
+def order_of(da, db):
+    far = db // 2 - db // 3
+    return far * (12 + da) + (1 - far) * (da * 3 + db - db // 3)
+
+
+def offsets_at(step):
+    far = step // 12
+    third = step % 3
+    return (1 - far) * (step // 3) + far * (step - 12), (1 - far) * (third + third // 2) + far * 2
+
+
 def score_kernel(
-    sel_ref, wanted_ref, g_ref, videos_ref, rows_ref, map_ref,
-    got_0, got_1, got_2, out, row, videos, sims,
-    got_sem, send_sem, recv_sem, self_sem, row_sem, video_sem,
+    q_ref, ids_ref, videos_ref, g_ref, rows_ref, map_ref,
+    got_0, got_1, got_2, out, row, videos, sims, table, sel, wanted, sel_ref, wanted_ref,
+    gather_send, gather_recv, local_sem, id_send, id_recv,
+    got_sem, send_sem, recv_sem, self_sem, row_sem, video_sem, table_sem,
 ):
     got = (got_0, got_1, got_2)
     chip, core = position()
-    load_videos = pltpu.make_async_copy(videos_ref, videos, video_sem)
-    load_videos.start()
+    me = device_at(chip, core)
     peers = [device_at(chip, core + 1)]
     for axis in range(3):
         for step in (1, 2, 3):
             for other in (0, 1):
                 peers.append(device_at(shifted(chip, axis, step), core + other))
+    load_videos = pltpu.make_async_copy(videos_ref, videos, video_sem)
+
+    def make_tables():
+        lane = lax.broadcasted_iota(jnp.int32, (1, Q_DEV * K), 1)
+        lanes = lax.broadcasted_iota(jnp.int32, (8, Q_DEV * K), 1)
+        places = lax.broadcasted_iota(jnp.int32, (8, Q_DEV * K), 0)
+
+        def one_source(source, carry):
+            ids = table[source]
+            key = lane * IDX_DEV + ids % IDX_DEV
+            mine = ids // IDX_DEV == me
+            low = jnp.min(jnp.where(mine, key, Q_DEV * K * IDX_DEV), axis=1, keepdims=True)
+            high = jnp.max(jnp.where(mine, key, 0), axis=1, keepdims=True)
+            wanted[source] = jnp.where(lane == 0, low % IDX_DEV, high % IDX_DEV)
+            return carry
+
+        lax.fori_loop(0, DEVICES, one_source, 0, unroll=8)
+
+        for t in range(3):
+            a, b, c = AXES[t]
+            spots = shifted(chip, c, places // 2)
+            target = device_at(spots, core + places % 2)
+
+            def one_block(step, carry):
+                da, db = offsets_at(step)
+                source = device_at(shifted(shifted(chip, a, da), b, db), core)
+                hit = jnp.broadcast_to(table[source] // IDX_DEV, (8, Q_DEV * K)) == target
+                first = jnp.min(jnp.where(hit, lanes // K, Q_DEV - 1), axis=1, keepdims=True)
+                last = jnp.max(jnp.where(hit, lanes // K, 0), axis=1, keepdims=True)
+                sel[t * BLOCKS + step] = jnp.where(lanes == 0, first, last)
+                return carry
+
+            lax.fori_loop(0, BLOCKS, one_block, 0, unroll=4)
+        moves = [
+            pltpu.make_async_copy(wanted, wanted_ref, table_sem.at[0]),
+            pltpu.make_async_copy(sel, sel_ref, table_sem.at[1]),
+        ]
+        for move in moves:
+            move.start()
+        for move in moves:
+            move.wait()
+
     greet(peers)
+    the_rest, all_sent = gather(
+        chip, core, q_ref, ids_ref, g_ref, table, make_tables,
+        gather_send, gather_recv, local_sem, id_send, id_recv,
+    )
+    load_videos.start()
 
     def fetch(block, t):
-        return pltpu.make_async_copy(
-            g_ref.at[t, block // 4, block % 4], got[t], got_sem.at[t]
-        )
+        da, db = offsets_at(block)
+        return pltpu.make_async_copy(g_ref.at[t, da, db], got[t], got_sem.at[t])
 
     def copies(block, t):
         slot = t * RING + block % RING
@@ -264,7 +327,7 @@
         slot = t * RING + block % RING
         for n in range(8):
             for rank in range(2):
-                pick = sel_ref[((t * BLOCKS + block) * 8 + n) * 2 + rank]
+                pick = sel_ref[t * BLOCKS + block, n, rank]
                 out[slot, n, rank] = got[t][pick]
         for copy in copies(block, t):
             copy.start()
@@ -280,16 +343,31 @@
         keep(block, t).wait()
         load_row(block, t).start()
 
+    def finish(at):
+        sim = sims[at]
+        best = sim[:, 0:F]
+        for s in range(1, R):
+            best = jnp.maximum(best, sim[:, s * F : (s + 1) * F])
+        total = best[0:F]
+        for r in range(1, R):
+            total = total + best[r * F : (r + 1) * F]
+        map_ref[at] = total * (1.0 / (math.sqrt(REGION_FEATURES) * R))
+
     def add_up(block, t):
         load_row(block, t).wait()
         a, b, c = AXES[t]
-        from_line = shifted(shifted(chip, a, block // 4), b, block % 4)
+        da, db = offsets_at(block)
+        from_line = shifted(shifted(chip, a, da), b, db)
 
         def one(n, carry):
-            source = device_at(shifted(from_line, c, 4 - n // 2), core + n % 2)
+            dc = (4 - n // 2) % 4
+            source = device_at(shifted(from_line, c, dc), core + n % 2)
+            now = block * 3 + t
+            next_one = order_of(db, dc) * 3 + (t + 1) % 3
+            other_one = order_of(dc, da) * 3 + (t + 2) % 3
             for rank in range(2):
                 at = source * 2 + rank
-                want = wanted_ref[at]
+                want = wanted_ref[source, 0, rank]
                 left = jnp.concatenate(
                     [row[t, n, rank, :, r * PART : (r + 1) * PART] for r in range(R)], axis=0
                 )
@@ -303,9 +381,15 @@
                 sims[at] += lax.dot_general(
                     left, right, (((1,), (1,)), ((), ())), preferred_element_type=jnp.float32
                 )
+
+            @pl.when(jnp.logical_and(now > next_one, now > other_one))
+            def _():
+                finish(source * 2)
+                finish(source * 2 + 1)
+
             return carry
 
-        lax.fori_loop(0, 8, one, 0)
+        lax.fori_loop(0, 8, one, 0, unroll=2)
 
     def one_block(block, carry):
         @pl.when(block == LAG)
@@ -313,6 +397,10 @@
             sims[...] = jnp.zeros_like(sims)
             load_videos.wait()
 
+        @pl.when(block == 11)
+        def _():
+            the_rest()
+
         for t in range(3):
             @pl.when(block < BLOCKS)
             def _():
@@ -333,18 +421,7 @@
         for block in range(BLOCKS - RING, BLOCKS):
             drain(block, t)
 
-    def finish(at, carry):
-        sim = sims[at]
-        best = sim[:, 0:F]
-        for s in range(1, R):
-            best = jnp.maximum(best, sim[:, s * F : (s + 1) * F])
-        total = best[0:F]
-        for r in range(1, R):
-            total = total + best[r * F : (r + 1) * F]
-        map_ref[at] = total * (1.0 / (math.sqrt(REGION_FEATURES) * R))
-        return carry
-
-    lax.fori_loop(0, SLOTS, finish, 0, unroll=4)
+    all_sent()
 
 
 def conv_same(x, w):
@@ -359,67 +436,19 @@
 
 
 def body(queries, index_videos, candidates, conv_one, conv_two, conv_three):
-    chip, core = position()
-    me = lax.axis_index("shard")
     pairs = Q_DEV * K
 
     flat = candidates.reshape(pairs)
-    gathered, everyone = pl.pallas_call(
-        gather_kernel,
+    _, _, maps = pl.pallas_call(
+        score_kernel,
         out_shape=(
             jax.ShapeDtypeStruct((3, SIDE, SIDE, Q_DEV, F, THIRD), jnp.bfloat16),
-            jax.ShapeDtypeStruct((DEVICES, 1, pairs), jnp.int32),
-        ),
-        in_specs=[pl.BlockSpec(memory_space=pl.ANY)] * 2,
-        out_specs=(pl.BlockSpec(memory_space=pl.ANY), pl.BlockSpec(memory_space=pl.ANY)),
-        scratch_shapes=[
-            pltpu.SemaphoreType.DMA((COPIES,)),
-            pltpu.SemaphoreType.DMA((COPIES,)),
-            pltpu.SemaphoreType.DMA((4, R)),
-            pltpu.SemaphoreType.DMA((10,)),
-            pltpu.SemaphoreType.DMA((10,)),
-        ],
-        compiler_params=pltpu.CompilerParams(collective_id=0, has_side_effects=True),
-        name="gather",
-    )(queries, flat.reshape(1, 1, pairs))
-    everyone = everyone.reshape(DEVICES, pairs)
-    holder = everyone // IDX_DEV
-    local = everyone % IDX_DEV
-    order = lax.broadcasted_iota(jnp.int32, (DEVICES, pairs), 1)
-    mine = holder == me
-    key = order * IDX_DEV + local
-    low = jnp.min(jnp.where(mine, key, pairs * IDX_DEV), axis=1)
-    high = jnp.max(jnp.where(mine, key, 0), axis=1)
-    wanted = jnp.stack([low % IDX_DEV, high % IDX_DEV], axis=1).reshape(SLOTS)
-
-    offset = jnp.arange(16, dtype=jnp.int32)
-    sources, targets = [], []
-    for a, b, c in AXES:
-        sources.append(device_at(shifted(shifted(chip, a, offset // 4), b, offset % 4), core))
-        line = jnp.arange(8, dtype=jnp.int32)
-        targets.append(device_at(shifted(chip, c, line // 2), core + line % 2))
-    sources = jnp.stack(sources)
-    targets = jnp.stack(targets)
-    asked = holder[sources]
-    hit = asked[:, :, None, :] == targets[:, None, :, None]
-    query_of = lax.broadcasted_iota(jnp.int32, (1, 1, 1, pairs), 3) // K
-    first_pick = jnp.min(jnp.where(hit, query_of, Q_DEV - 1), axis=3)
-    last_pick = jnp.max(jnp.where(hit, query_of, 0), axis=3)
-    sel = jnp.stack([first_pick, last_pick], axis=3).reshape(3 * 16 * 8 * 2)
-
-    _, maps = pl.pallas_call(
-        score_kernel,
-        out_shape=(
             jax.ShapeDtypeStruct((3, BLOCKS, 8, 2, F, THIRD), jnp.bfloat16),
             jax.ShapeDtypeStruct((SLOTS, F, F), jnp.float32),
         ),
-        in_specs=[
-            pl.BlockSpec(memory_space=pltpu.SMEM),
-            pl.BlockSpec(memory_space=pltpu.SMEM),
+        in_specs=[pl.BlockSpec(memory_space=pl.ANY)] * 3,
+        out_specs=(
             pl.BlockSpec(memory_space=pl.ANY),
-            pl.BlockSpec(memory_space=pl.ANY),
-        ],
-        out_specs=(
             pl.BlockSpec(memory_space=pl.ANY),
             pl.BlockSpec(memory_space=pltpu.VMEM),
         ),
@@ -431,18 +460,29 @@
             pltpu.VMEM((3, 8, 2, F, THIRD), jnp.bfloat16),
             pltpu.VMEM((IDX_DEV, F, WIDTH), jnp.bfloat16),
             pltpu.VMEM((SLOTS, F * R, F * R), jnp.float32),
+            pltpu.VMEM((DEVICES, 1, pairs), jnp.int32),
+            pltpu.VMEM((3 * BLOCKS, 8, pairs), jnp.int32),
+            pltpu.VMEM((DEVICES, 1, pairs), jnp.int32),
+            pltpu.SMEM((3 * BLOCKS, 8, pairs), jnp.int32),
+            pltpu.SMEM((DEVICES, 1, pairs), jnp.int32),
+            pltpu.SemaphoreType.DMA((COPIES,)),
+            pltpu.SemaphoreType.DMA((COPIES,)),
+            pltpu.SemaphoreType.DMA((4, R)),
+            pltpu.SemaphoreType.DMA((10,)),
+            pltpu.SemaphoreType.DMA((10,)),
             pltpu.SemaphoreType.DMA((3,)),
             pltpu.SemaphoreType.DMA((3 * RING, 8)),
             pltpu.SemaphoreType.DMA((3, BLOCKS, 8)),
             pltpu.SemaphoreType.DMA((3 * RING,)),
             pltpu.SemaphoreType.DMA((3,)),
             pltpu.SemaphoreType.DMA,
+            pltpu.SemaphoreType.DMA((2,)),
         ],
         compiler_params=pltpu.CompilerParams(
-            collective_id=1, has_side_effects=True, vmem_limit_bytes=56 << 20
+            collective_id=0, has_side_effects=True, vmem_limit_bytes=56 << 20
         ),
         name="score",
-    )(sel, wanted, gathered, index_videos)
+    )(queries, flat.reshape(1, 1, pairs), index_videos)
 
     frame_map = maps.reshape(SLOTS, 1, F, F).astype(jnp.bfloat16)
     first = pool_two(jax.nn.relu(conv_same(frame_map, conv_one))).astype(jnp.bfloat16)

time: 347 us -> 334 us (0.963)
  Pallas kernels: 318 us -> 309 us
  other arithmetic: 5.72 us -> 1.95 us
    pallas_call x2 -> x1, Pallas kernels: 318 us -> 309 us  [body(): pl.pallas_call(score_kernel, out_shape=(jax.ShapeDtypeStruct((3, SIDE, SI...]
where the time goes in v3:
time: 334 us; the launch traced here: 333 us
  Pallas kernels  309 us (93%)
  waiting for transfers between devices  9.33 us (3%)
  starting transfers between devices  8.3 us (2%)
  local copies, waits for them, and re-layouts  3.65 us (1%)
    pallas_call x1, Pallas kernels, body(): pl.pallas_call(score_kernel, out_shape=(jax.ShapeDtypeStruct((3, SIDE, SI...  309 us
    all_to_all x1, waiting for transfers between devices, body(): lax.all_to_all(scores.reshape(DEVICES, 2), 'shard', split_axis=0, concat_...  9.33 us
    all_to_all x1, starting transfers between devices, body(): lax.all_to_all(scores.reshape(DEVICES, 2), 'shard', split_axis=0, concat_...  8.3 us
  transfers between devices with their start and end apart: 1, of which 1 were waited for; matrix products, arithmetic and copies ran while one was open for 0% of the time, Pallas kernels for 0%

profile of v3, /device:TPU:1, one launch (start us, length us, event | category | flops | bytes accessed | tf_op | source)
XLA Modules:
  0.0 333.5 jit_solution(4983963535057850049)
XLA Ops:
  0.0 0.0 copy-start
  0.0 0.8 copy.32
  0.8 0.6 reshape_reshape.3.ids_ref
  1.4 308.8 %score.1 = (bf16[3,4,4,16,8,3200]{5,4,3,2,1,0:T(8,128)(2,1)}, bf16[3,16,8,2,8,3200]{5,4,3,2,1,0:T(8,128)(2,1)}, f32[256,8,8]{2,1,0:T(8,128)}) custom-call(bf16[16,8,9600]{2,1,0:T(8,128)(2,1)} %q_ref.1, s32[1,1,128]{2,1,0:T(1,128)} %reshape_reshape.3.ids_ref, bf16[128,8,9600]{2,1,0:T(8,128)(2,1)} %videos_ref.1), custom_call_target="tpu_custom_call" | custom-call | tf_op jit(solution)/shard_map/score/pallas_call | solution.py:442
  310.2 1.3 convert_bitcast_fusion
  311.5 0.0 copy-start.2
  311.5 0.4 copy.34
  311.9 0.0 copy-done.1
  311.9 0.5 convolution_maximum_fusion
  312.5 0.2 reduce_max.27
  312.7 0.0 copy-done
  312.7 0.6 convolution_maximum_fusion.1
  313.3 0.1 reduce_max.28
  313.4 0.0 copy-done.2
  313.4 0.2 fusion
  313.7 0.8 div.26
  314.4 8.3 %all-to-all-start = ((f32[128,1,2]{2,1,0:T(1,128)}), f32[128,1,2]{2,1,0:T(1,128)S(1)}, u32[]{:S(2)}, u32[]{:S(2)}) async-start(f32[128,1,2]{2,1,0:T(1,128)} %bitcast.3), calls=%async_computation | async-start | bytes 131072 | tf_op jit(solution)/shard_map/all_to_all | solution.py:493
  322.8 0.1 reshape.93
  322.9 0.2 fusion.4
  323.0 9.3 %all-to-all-done = f32[128,1,2]{2,1,0:T(1,128)S(1)} async-done(((f32[128,1,2]{2,1,0:T(1,128)}), f32[128,1,2]{2,1,0:T(1,128)S(1)}, u32[]{:S(2)}, u32[]{:S(2)}) %all-to-all-start) | async-done | bytes 1056 | tf_op jit(solution)/shard_map/all_to_all | solution.py:493
  332.4 0.2 slice_reduce_fusion
  332.5 0.2 select_reduce_fusion
  332.7 0.1 select_n.32
  332.8 0.7 copy.38
  (6 shorter events, 0.1 us)
Async XLA Ops:
  0.0 312.7 %copy-start = (bf16[64,32,3,3]{0,1,3,2:T(8,128)(2,1)S(1)}, bf16[64,32,3,3]{0,1,3,2:T(8,128)(2,1)}, u32[]{:S(2)}) copy-start(bf16[64,32,3,3]{0,1,3,2:T(8,128)(2,1)} %param.10) | copy-start | bytes 110596
  1.4 310.5 %copy-start.1 = (bf16[32,1,3,3]{0,3,2,1:T(4,128)(2,1)S(1)}, bf16[32,1,3,3]{0,3,2,1:T(4,128)(2,1)}, u32[]{:S(2)}) copy-start(bf16[32,1,3,3]{0,3,2,1:T(4,128)(2,1)} %param.9) | copy-start | bytes 1732
  311.5 1.9 copy-start.2
  314.4 17.9 %all-to-all-start = ((f32[128,1,2]{2,1,0:T(1,128)}), f32[128,1,2]{2,1,0:T(1,128)S(1)}, u32[]{:S(2)}, u32[]{:S(2)}) async-start(f32[128,1,2]{2,1,0:T(1,128)} %bitcast.3), calls=%async_computation | async-start | bytes 131072 | tf_op jit(solution)/shard_map/all_to_all | solution.py:493

commit v4 on v3

--- a/solution.py
+++ b/solution.py
@@ -13,8 +13,8 @@
 R = 5
 REGION_FEATURES = 1920
 WIDTH = R * REGION_FEATURES
-THIRD = WIDTH // 3
 PART = REGION_FEATURES // 3
+FR = F * R
 SIDE = 4
 Q_DEV = 16
 K = 8
@@ -57,7 +57,7 @@
         for r in range(R):
             copy = pltpu.make_async_copy(
                 q_ref.at[:, :, pl.ds(r * REGION_FEATURES + t * PART, PART)],
-                g_ref.at[t, 0, 0, :, :, pl.ds(r * PART, PART)],
+                g_ref.at[t, 0, 0, :, pl.ds(r * F, F)],
                 local_sem.at[t, r],
             )
             own.append(copy)
@@ -75,7 +75,7 @@
             number = len(started)
             copy = pltpu.make_async_remote_copy(
                 src_ref=q_ref.at[:, :, pl.ds(r * REGION_FEATURES + t * PART, PART)],
-                dst_ref=g_ref.at[t, to_a, to_b, :, :, pl.ds(r * PART, PART)],
+                dst_ref=g_ref.at[t, to_a, to_b, :, pl.ds(r * F, F)],
                 send_sem=send_sem.at[number],
                 recv_sem=recv_sem.at[number],
                 device_id=(near[axis, step],),
@@ -207,9 +207,14 @@
 BLOCKS = SIDE * SIDE
 
 
-def order_of(da, db):
-    far = db // 2 - db // 3
-    return far * (12 + da) + (1 - far) * (da * 3 + db - db // 3)
+def frame_map(sim):
+    best = sim[:, 0:F]
+    for s in range(1, R):
+        best = jnp.maximum(best, sim[:, s * F : (s + 1) * F])
+    total = best[0:F]
+    for r in range(1, R):
+        total = total + best[r * F : (r + 1) * F]
+    return total * (1.0 / (math.sqrt(REGION_FEATURES) * R))
 
 
 def offsets_at(step):
@@ -232,7 +237,14 @@
         for step in (1, 2, 3):
             for other in (0, 1):
                 peers.append(device_at(shifted(chip, axis, step), core + other))
-    load_videos = pltpu.make_async_copy(videos_ref, videos, video_sem)
+    load_videos = [
+        pltpu.make_async_copy(
+            videos_ref.at[:, :, pl.ds(r * REGION_FEATURES, REGION_FEATURES)],
+            videos.at[:, pl.ds(r * F, F)],
+            video_sem.at[r],
+        )
+        for r in range(R)
+    ]
 
     def make_tables():
         lane = lax.broadcasted_iota(jnp.int32, (1, Q_DEV * K), 1)
@@ -279,7 +291,8 @@
         chip, core, q_ref, ids_ref, g_ref, table, make_tables,
         gather_send, gather_recv, local_sem, id_send, id_recv,
     )
-    load_videos.start()
+    for copy in load_videos:
+        copy.start()
 
     def fetch(block, t):
         da, db = offsets_at(block)
@@ -343,59 +356,32 @@
         keep(block, t).wait()
         load_row(block, t).start()
 
-    def finish(at):
-        sim = sims[at]
-        best = sim[:, 0:F]
-        for s in range(1, R):
-            best = jnp.maximum(best, sim[:, s * F : (s + 1) * F])
-        total = best[0:F]
-        for r in range(1, R):
-            total = total + best[r * F : (r + 1) * F]
-        map_ref[at] = total * (1.0 / (math.sqrt(REGION_FEATURES) * R))
-
     def add_up(block, t):
         load_row(block, t).wait()
         a, b, c = AXES[t]
         da, db = offsets_at(block)
         from_line = shifted(shifted(chip, a, da), b, db)
 
-        def one(n, carry):
-            dc = (4 - n // 2) % 4
-            source = device_at(shifted(from_line, c, dc), core + n % 2)
-            now = block * 3 + t
-            next_one = order_of(db, dc) * 3 + (t + 1) % 3
-            other_one = order_of(dc, da) * 3 + (t + 2) % 3
+        for n in range(8):
+            source = device_at(shifted(from_line, c, (4 - n // 2) % 4), core + n % 2)
             for rank in range(2):
                 at = source * 2 + rank
                 want = wanted_ref[source, 0, rank]
-                left = jnp.concatenate(
-                    [row[t, n, rank, :, r * PART : (r + 1) * PART] for r in range(R)], axis=0
+                sim = sims[at] + lax.dot_general(
+                    row[t, n, rank],
+                    videos[want, :, pl.ds(t * PART, PART)],
+                    (((1,), (1,)), ((), ())),
+                    preferred_element_type=jnp.float32,
                 )
-                right = jnp.concatenate(
-                    [
-                        videos[want, :, pl.ds(s * REGION_FEATURES + t * PART, PART)]
-                        for s in range(R)
-                    ],
-                    axis=0,
-                )
-                sims[at] += lax.dot_general(
-                    left, right, (((1,), (1,)), ((), ())), preferred_element_type=jnp.float32
-                )
-
-            @pl.when(jnp.logical_and(now > next_one, now > other_one))
-            def _():
-                finish(source * 2)
-                finish(source * 2 + 1)
-
-            return carry
-
-        lax.fori_loop(0, 8, one, 0, unroll=2)
+                sims[at] = sim
+                map_ref[at] = frame_map(sim)
 
     def one_block(block, carry):
         @pl.when(block == LAG)
         def _():
             sims[...] = jnp.zeros_like(sims)
-            load_videos.wait()
+            for copy in load_videos:
+                copy.wait()
 
         @pl.when(block == 11)
         def _():
@@ -442,8 +428,8 @@
     _, _, maps = pl.pallas_call(
         score_kernel,
         out_shape=(
-            jax.ShapeDtypeStruct((3, SIDE, SIDE, Q_DEV, F, THIRD), jnp.bfloat16),
-            jax.ShapeDtypeStruct((3, BLOCKS, 8, 2, F, THIRD), jnp.bfloat16),
+            jax.ShapeDtypeStruct((3, SIDE, SIDE, Q_DEV, FR, PART), jnp.bfloat16),
+            jax.ShapeDtypeStruct((3, BLOCKS, 8, 2, FR, PART), jnp.bfloat16),
             jax.ShapeDtypeStruct((SLOTS, F, F), jnp.float32),
         ),
         in_specs=[pl.BlockSpec(memory_space=pl.ANY)] * 3,
@@ -453,13 +439,13 @@
             pl.BlockSpec(memory_space=pltpu.VMEM),
         ),
         scratch_shapes=[
-            pltpu.VMEM((Q_DEV, F, THIRD), jnp.bfloat16),
-            pltpu.VMEM((Q_DEV, F, THIRD), jnp.bfloat16),
-            pltpu.VMEM((Q_DEV, F, THIRD), jnp.bfloat16),
-            pltpu.VMEM((3 * RING, 8, 2, F, THIRD), jnp.bfloat16),
-            pltpu.VMEM((3, 8, 2, F, THIRD), jnp.bfloat16),
-            pltpu.VMEM((IDX_DEV, F, WIDTH), jnp.bfloat16),
-            pltpu.VMEM((SLOTS, F * R, F * R), jnp.float32),
+            pltpu.VMEM((Q_DEV, FR, PART), jnp.bfloat16),
+            pltpu.VMEM((Q_DEV, FR, PART), jnp.bfloat16),
+            pltpu.VMEM((Q_DEV, FR, PART), jnp.bfloat16),
+            pltpu.VMEM((3 * RING, 8, 2, FR, PART), jnp.bfloat16),
+            pltpu.VMEM((3, 8, 2, FR, PART), jnp.bfloat16),
+            pltpu.VMEM((IDX_DEV, FR, REGION_FEATURES), jnp.bfloat16),
+            pltpu.VMEM((SLOTS, FR, FR), jnp.float32),
             pltpu.VMEM((DEVICES, 1, pairs), jnp.int32),
             pltpu.VMEM((3 * BLOCKS, 8, pairs), jnp.int32),
             pltpu.VMEM((DEVICES, 1, pairs), jnp.int32),
@@ -475,7 +461,7 @@
             pltpu.SemaphoreType.DMA((3, BLOCKS, 8)),
             pltpu.SemaphoreType.DMA((3 * RING,)),
             pltpu.SemaphoreType.DMA((3,)),
-            pltpu.SemaphoreType.DMA,
+            pltpu.SemaphoreType.DMA((R,)),
             pltpu.SemaphoreType.DMA((2,)),
         ],
         compiler_params=pltpu.CompilerParams(
@@ -484,8 +470,8 @@
         name="score",
     )(queries, flat.reshape(1, 1, pairs), index_videos)
 
-    frame_map = maps.reshape(SLOTS, 1, F, F).astype(jnp.bfloat16)
-    first = pool_two(jax.nn.relu(conv_same(frame_map, conv_one))).astype(jnp.bfloat16)
+    frames = maps.reshape(SLOTS, 1, F, F).astype(jnp.bfloat16)
+    first = pool_two(jax.nn.relu(conv_same(frames, conv_one))).astype(jnp.bfloat16)
     second = pool_two(jax.nn.relu(conv_same(first, conv_two))).astype(jnp.bfloat16)
     final = conv_same(second, conv_three)[:, 0]
     scores = jnp.mean(jnp.max(jnp.clip(final, -1.0, 1.0), axis=2), axis=1)

time: 334 us -> 322 us (0.964)
  Pallas kernels: 309 us -> 300 us
    pallas_call x1, Pallas kernels: 309 us -> 300 us  [body(): pl.pallas_call(score_kernel, out_shape=(jax.ShapeDtypeStruct((3, SIDE, SI...]
where the time goes in v4:
time: 322 us
  Pallas kernels  300 us (93%)
  waiting for transfers between devices  9.33 us (3%)
  starting transfers between devices  5.74 us (2%)
  local copies, waits for them, and re-layouts  3.65 us (1%)
    pallas_call x1, Pallas kernels, body(): pl.pallas_call(score_kernel, out_shape=(jax.ShapeDtypeStruct((3, SIDE, SI...  300 us
    all_to_all x1, waiting for transfers between devices, body(): lax.all_to_all(scores.reshape(DEVICES, 2), 'shard', split_axis=0, concat_...  9.33 us
  transfers between devices with their start and end apart: 1, of which 1 were waited for; matrix products, arithmetic and copies ran while one was open for 0% of the time, Pallas kernels for 0%

profile of v4, /device:TPU:1, one launch (start us, length us, event | category | flops | bytes accessed | tf_op | source)
XLA Modules:
  0.0 321.8 jit_solution(16179505083823791417)
XLA Ops:
  0.0 0.0 copy-start
  0.0 0.8 copy.32
  0.8 0.6 reshape_reshape.3.ids_ref
  1.4 299.6 %score.1 = (bf16[3,4,4,16,40,640]{5,4,3,2,1,0:T(8,128)(2,1)}, bf16[3,16,8,2,40,640]{5,4,3,2,1,0:T(8,128)(2,1)}, f32[256,8,8]{2,1,0:T(8,128)}) custom-call(bf16[16,8,9600]{2,1,0:T(8,128)(2,1)} %q_ref.1, s32[1,1,128]{2,1,0:T(1,128)} %reshape_reshape.3.ids_ref, bf16[128,8,9600]{2,1,0:T(8,128)(2,1)} %videos_ref.1), custom_call_target="tpu_custom_call" | custom-call | tf_op jit(solution)/shard_map/score/pallas_call | solution.py:428
  301.0 1.3 convert_bitcast_fusion
  302.3 0.0 copy-start.2
  302.3 0.4 copy.34
  302.7 0.0 copy-done.1
  302.8 0.5 convolution_maximum_fusion
  303.3 0.2 reduce_max.27
  303.5 0.0 copy-done
  303.5 0.6 convolution_maximum_fusion.1
  304.1 0.1 reduce_max.28
  304.2 0.0 copy-done.2
  304.3 0.2 fusion
  304.5 0.8 div.26
  305.3 5.7 %all-to-all-start = ((f32[128,1,2]{2,1,0:T(1,128)}), f32[128,1,2]{2,1,0:T(1,128)S(1)}, u32[]{:S(2)}, u32[]{:S(2)}) async-start(f32[128,1,2]{2,1,0:T(1,128)} %bitcast.3), calls=%async_computation | async-start | bytes 131072 | tf_op jit(solution)/shard_map/all_to_all | solution.py:479
  311.0 0.1 reshape.93
  311.1 0.2 fusion.4
  311.3 9.3 %all-to-all-done = f32[128,1,2]{2,1,0:T(1,128)S(1)} async-done(((f32[128,1,2]{2,1,0:T(1,128)}), f32[128,1,2]{2,1,0:T(1,128)S(1)}, u32[]{:S(2)}, u32[]{:S(2)}) %all-to-all-start) | async-done | bytes 1056 | tf_op jit(solution)/shard_map/all_to_all | solution.py:479
  320.6 0.2 slice_reduce_fusion
  320.8 0.2 select_reduce_fusion
  321.0 0.1 select_n.32
  321.1 0.7 copy.38
  (6 shorter events, 0.1 us)
Async XLA Ops:
  0.0 303.5 %copy-start = (bf16[64,32,3,3]{0,1,3,2:T(8,128)(2,1)S(1)}, bf16[64,32,3,3]{0,1,3,2:T(8,128)(2,1)}, u32[]{:S(2)}) copy-start(bf16[64,32,3,3]{0,1,3,2:T(8,128)(2,1)} %param.10) | copy-start | bytes 110596
  1.4 301.4 %copy-start.1 = (bf16[32,1,3,3]{0,3,2,1:T(4,128)(2,1)S(1)}, bf16[32,1,3,3]{0,3,2,1:T(4,128)(2,1)}, u32[]{:S(2)}) copy-start(bf16[32,1,3,3]{0,3,2,1:T(4,128)(2,1)} %param.9) | copy-start | bytes 1732
  302.3 1.9 copy-start.2
  305.3 15.4 %all-to-all-start = ((f32[128,1,2]{2,1,0:T(1,128)}), f32[128,1,2]{2,1,0:T(1,128)S(1)}, u32[]{:S(2)}, u32[]{:S(2)}) async-start(f32[128,1,2]{2,1,0:T(1,128)} %bitcast.3), calls=%async_computation | async-start | bytes 131072 | tf_op jit(solution)/shard_map/all_to_all | solution.py:479

commit v5 on v4

--- a/solution.py
+++ b/solution.py
@@ -408,6 +408,47 @@
             drain(block, t)
 
     all_sent()
+
+
+def return_kernel(give_ref, out_ref, middle, send_sem, recv_sem, own_sem):
+    chip, core = position()
+    z, x, y = chip
+    pillar = z * 4 + x
+    spot = y * 2 + core
+    far = [(step, (pillar + step) % 16) for step in range(1, 16)]
+    near = [(step, (spot + step) % 8) for step in range(1, 8)]
+    greet([at * 8 + spot for _, at in far] + [pillar * 8 + at for _, at in near])
+
+    def hop(first, moves, own_source, target):
+        made = []
+        for i, (source, peer) in enumerate(moves):
+            made.append(
+                pltpu.make_async_remote_copy(
+                    src_ref=source,
+                    dst_ref=target,
+                    send_sem=send_sem.at[first + i],
+                    recv_sem=recv_sem.at[first + i],
+                    device_id=(peer,),
+                    device_id_type=MESH,
+                )
+            )
+        own = pltpu.make_async_copy(own_source, target, own_sem)
+        for copy in made:
+            copy.start()
+        own.start()
+        own.wait()
+        for copy in made:
+            copy.wait_recv()
+        return made
+
+    sent = hop(
+        0, [(give_ref.at[at], at * 8 + spot) for _, at in far], give_ref.at[pillar], middle.at[pillar]
+    )
+    sent += hop(
+        15, [(middle.at[:, at], pillar * 8 + at) for _, at in near], middle.at[:, spot], out_ref.at[spot]
+    )
+    for copy in sent:
+        copy.wait_send()
 
 
 def conv_same(x, w):
@@ -476,12 +517,28 @@
     final = conv_same(second, conv_three)[:, 0]
     scores = jnp.mean(jnp.max(jnp.clip(final, -1.0, 1.0), axis=2), axis=1)
 
-    back = lax.all_to_all(scores.reshape(DEVICES, 2), "shard", split_axis=0, concat_axis=0, tiled=True)
+    give = jnp.pad(scores.reshape(16, 8, 1, 2), ((0, 0), (0, 0), (0, 0), (0, pairs - 2)))
+    back = pl.pallas_call(
+        return_kernel,
+        out_shape=jax.ShapeDtypeStruct((8, 16, 1, pairs), jnp.float32),
+        in_specs=[pl.BlockSpec(memory_space=pltpu.VMEM)],
+        out_specs=pl.BlockSpec(memory_space=pltpu.VMEM),
+        scratch_shapes=[
+            pltpu.VMEM((16, 8, 1, pairs), jnp.float32),
+            pltpu.SemaphoreType.DMA((22,)),
+            pltpu.SemaphoreType.DMA((22,)),
+            pltpu.SemaphoreType.DMA,
+        ],
+        compiler_params=pltpu.CompilerParams(collective_id=1, has_side_effects=True),
+        name="give_back",
+    )(give)
+    back = back.reshape(DEVICES, pairs)[:, :2]
     my_holder = flat // IDX_DEV
     same = my_holder[:, None] == my_holder[None, :]
     earlier = jnp.arange(pairs)[None, :] < jnp.arange(pairs)[:, None]
     second_one = jnp.any(same & earlier, axis=1)
-    to_me = my_holder[:, None] == jnp.arange(DEVICES)[None, :]
+    at = my_holder % 8 * 16 + my_holder // 8
+    to_me = at[:, None] == jnp.arange(DEVICES)[None, :]
     score_first = jnp.sum(jnp.where(to_me, back[None, :, 0], 0.0), axis=1)
     score_last = jnp.sum(jnp.where(to_me, back[None, :, 1], 0.0), axis=1)
     return jnp.where(second_one, score_last, score_first).reshape(Q_DEV, K)

time: 322 us -> 321 us (level)
  Pallas kernels: 300 us -> 312 us
  waiting for transfers between devices: 9.33 us -> 0 us
  starting transfers between devices: 5.74 us -> 0 us
    pallas_call x0 -> x1, Pallas kernels: none -> 12.7 us  [body(): pl.pallas_call(return_kernel, out_shape=jax.ShapeDtypeStruct((8, 16, 1, p...]
    all_to_all x1 -> x0, waiting for transfers between devices: 9.33 us -> none  [body(): lax.all_to_all(scores.reshape(DEVICES, 2), 'shard', split_axis=0, concat_...]
    all_to_all x1 -> x0, starting transfers between devices: 5.74 us -> none  [body(): lax.all_to_all(scores.reshape(DEVICES, 2), 'shard', split_axis=0, concat_...]
  transfers between devices with their start and end apart: 1 -> 0, of which waited for: 1 -> 0; matrix products, arithmetic and copies ran while one was open for 0% -> 0% of each run, Pallas kernels for 0% -> 0%
where the time goes in v5:
time: 321 us; the launch traced here: 320 us
  Pallas kernels  312 us (97%)
  local copies, waits for them, and re-layouts  4.66 us (1%)
    pallas_call x1, Pallas kernels, body(): pl.pallas_call(score_kernel, out_shape=(jax.ShapeDtypeStruct((3, SIDE, SI...  300 us
    pallas_call x1, Pallas kernels, body(): pl.pallas_call(return_kernel, out_shape=jax.ShapeDtypeStruct((8, 16, 1, p...  12.7 us

profile of v5, /device:TPU:1, one launch (start us, length us, event | category | flops | bytes accessed | tf_op | source)
XLA Modules:
  0.0 320.4 jit_solution(11439930783822785785)
XLA Ops:
  0.0 0.0 copy-start
  0.0 0.8 copy.33
  0.8 0.1 reshape.130
  0.9 0.2 fusion.4
  1.1 0.6 reshape_reshape.3.ids_ref
  1.7 299.6 %score.1 = (bf16[3,4,4,16,40,640]{5,4,3,2,1,0:T(8,128)(2,1)}, bf16[3,16,8,2,40,640]{5,4,3,2,1,0:T(8,128)(2,1)}, f32[256,8,8]{2,1,0:T(8,128)}) custom-call(bf16[16,8,9600]{2,1,0:T(8,128)(2,1)} %q_ref.1, s32[1,1,128]{2,1,0:T(1,128)} %reshape_reshape.3.ids_ref, bf16[128,8,9600]{2,1,0:T(8,128)(2,1)} %videos_ref.1), custom_call_target="tpu_custom_call" | custom-call | tf_op jit(solution)/shard_map/score/pallas_call | solution.py:469
  301.3 1.3 convert_bitcast_fusion
  302.6 0.0 copy-start.2
  302.6 0.4 copy.35
  303.1 0.0 copy-done.1
  303.1 0.5 convolution_maximum_fusion
  303.6 0.2 reduce_max.27
  303.8 0.6 convolution_maximum_fusion.1
  304.5 0.1 reduce_max.28
  304.6 0.2 fusion
  304.8 0.1 div.40
  305.0 0.7 pad.4.give_ref
  305.6 12.7 %give_back.1 = f32[8,16,1,128]{3,2,1,0:T(1,128)} custom-call(f32[16,8,1,128]{3,2,1,0:T(1,128)} %pad.4.give_ref), custom_call_target="tpu_custom_call" | custom-call | tf_op jit(solution)/shard_map/give_back/pallas_call | solution.py:521
  318.3 1.0 fusion.9
  319.3 0.1 copy.43
  319.4 0.1 copy.42
  319.5 0.2 select_reduce_fusion
  319.7 0.1 select_n.55
  319.8 0.7 copy.41
  (8 shorter events, 0.1 us)
Async XLA Ops:
  0.0 303.8 %copy-start = (bf16[64,32,3,3]{0,1,3,2:T(8,128)(2,1)S(1)}, bf16[64,32,3,3]{0,1,3,2:T(8,128)(2,1)}, u32[]{:S(2)}) copy-start(bf16[64,32,3,3]{0,1,3,2:T(8,128)(2,1)} %param.10) | copy-start | bytes 110596
  1.7 301.4 %copy-start.1 = (bf16[32,1,3,3]{0,3,2,1:T(4,128)(2,1)S(1)}, bf16[32,1,3,3]{0,3,2,1:T(4,128)(2,1)}, u32[]{:S(2)}) copy-start(bf16[32,1,3,3]{0,3,2,1:T(4,128)(2,1)} %param.9) | copy-start | bytes 1732
  302.6 1.9 copy-start.2
